TPU v7x, 32 devices: a whole 2x2x4 slice. The times are simulated.
32 devices in a mesh: lat: 4 (over z), lev: 8 (over y, x, core).
Axes of the slice: x: 2, y: 2, z: 4, core: 2. Of those that a mesh axis runs over, the one named last changes fastest.
Arguments:
- spec_in: bfloat16 [8, 2, 8, 2560], P('lat', None, None, 'lev'), may hold values from -6 to 6
- legendre: bfloat16 [8, 2560, 2560], P('lat', 'lev'), may hold values from -0.125 to 0.125
- pattern: int32 [8, 20, 20], P('lat'), may hold values from 0 to 1, as said below
- deal_list: int32 [8], replicated, may hold values from 0 to 2559, as said below
- circle_lengths: int32 [2560], replicated, may hold values from 12 to 10256, as said below
- mixing: bfloat16 [8, 8], replicated, may hold values from -2 to 2
Outputs:
- spec_out: float32 [8, 2, 8, 2560], P('lat', None, None, 'lev')
Inputs may be any that keep to these rules, and one draw needn't show every extreme that they name: `deal_list`: distinct wavenumbers; 0 and 2559 are always among them. pattern[m, a, b] is 1 exactly when b * 128 <= 2559 - deal_list[m] and a >= (deal_list[m] * 20) // 5120, else 0. `circle_lengths`: multiples of 4; row j holds a value between 20 + 4 j - 4 (j // 2 + 2) and 20 + 4 j, and the last row exactly 20 + 4 (2559).
All inputs are finite; a program needn't handle non-finite values.
Results may differ from a plain program's by a relative error of at most 0.0026.
Values may be sent and summed in bfloat16 or wider, within the bound.
A program may use at most 64 MiB of HBM per device.

v0:
```python
import math

import jax
import jax.numpy as jnp
from jax import lax
from jax.sharding import PartitionSpec as P

BLK = 128


def local(spec_in, legendre, pattern, deal_list, circle_lengths, mixing):
    lat_index = lax.axis_index("lat")
    lev_index = lax.axis_index("lev")
    lat_count = lax.axis_size("lat")
    lev_count = lax.axis_size("lev")
    slot_count, local_cols, half_lat = legendre.shape
    fields = spec_in.shape[2]
    wave_count = deal_list.shape[0]
    col_blocks = pattern.shape[2]
    local_rows = half_lat // (lat_count * lev_count)
    lon_count = 20 + 4 * (half_lat - 1)
    global_cols = lev_index * local_cols + jnp.arange(local_cols, dtype=jnp.int32)
    parity = (1 - 2 * (global_cols % 2)).astype(jnp.float32)
    chooser = (
        global_cols[None, :] // BLK == jnp.arange(col_blocks, dtype=jnp.int32)[:, None]
    ).astype(jnp.bfloat16)
    row_live = jnp.repeat(pattern, BLK, axis=1).astype(jnp.bfloat16)
    block_live = jnp.einsum("sjb,bk->skj", row_live, chooser, preferred_element_type=jnp.float32)
    masked = legendre * block_live.astype(jnp.bfloat16)
    signed = (spec_in.astype(jnp.float32) * parity).astype(jnp.bfloat16)
    stacked = jnp.stack([spec_in, signed], axis=1)
    partial_value = jnp.einsum(
        "skj,shrfk->shrfj", masked, stacked, preferred_element_type=jnp.float32
    )
    summed = lax.psum_scatter(partial_value, "lev", scatter_dimension=3, tiled=True).astype(
        jnp.bfloat16
    )
    arranged = summed.reshape(
        slot_count, 2, 2, fields // lev_count, lev_count, lat_count, local_rows
    )
    fourier = lax.all_to_all(
        lax.all_to_all(arranged, "lat", split_axis=5, concat_axis=0, tiled=True),
        "lev",
        split_axis=4,
        concat_axis=3,
        tiled=True,
    )
    fourier = fourier.reshape(wave_count, 2, 2, fields, local_rows)
    row_ids = (
        lev_index * (half_lat // lev_count)
        + lat_index * local_rows
        + jnp.arange(local_rows, dtype=jnp.int32)
    )
    synth_scale = (2.0 * wave_count) ** (-0.5)
    positions = jnp.arange(lon_count, dtype=jnp.int32)

    def row_work(inputs):
        fourier_row, row_id = inputs
        length = circle_lengths[row_id]
        phases = deal_list[:, None] * positions[None, :] % length
        angles = phases.astype(jnp.float32) * (2.0 * math.pi) / length.astype(jnp.float32)
        inside = positions[None, :] < length
        cosine_table = jnp.where(inside, jnp.cos(angles), 0.0).astype(jnp.bfloat16)
        sine_table = jnp.where(inside, jnp.sin(angles), 0.0).astype(jnp.bfloat16)
        phases_table = jnp.concatenate([cosine_table, -sine_table], axis=0)
        coeffs = jnp.transpose(fourier_row, (1, 3, 2, 0)).reshape(2 * fields, 2 * wave_count)
        grid_values = (
            jnp.dot(coeffs, phases_table, preferred_element_type=jnp.float32) * synth_scale
        ).astype(jnp.bfloat16)
        grid_levels = grid_values.reshape(2, fields, lon_count)
        mixed_sum = jnp.einsum(
            "fg,hgl->hfl", mixing, grid_levels, preferred_element_type=jnp.float32
        )
        column = (
            (grid_levels.astype(jnp.float32) + jnp.tanh(mixed_sum))
            .astype(jnp.bfloat16)
            .reshape(2 * fields, lon_count)
        )
        weight = jnp.sin(math.pi * (row_id.astype(jnp.float32) + 0.5) / (2 * half_lat)) / jnp.sqrt(
            length.astype(jnp.float32)
        )
        analysis = lax.dot_general(
            column, phases_table, (((1,), (1,)), ((), ())), preferred_element_type=jnp.float32
        )
        analysis = (analysis * weight).astype(jnp.bfloat16)
        return jnp.transpose(analysis.reshape(2, fields, 2, wave_count), (3, 0, 2, 1))

    analysed = lax.map(row_work, (jnp.moveaxis(fourier, 4, 0), row_ids))
    analysed = jnp.moveaxis(analysed, 0, 4)
    arranged = analysed.reshape(wave_count, 2, 2, fields, 1, 1, local_rows)
    returned = lax.all_to_all(
        lax.all_to_all(arranged, "lat", split_axis=0, concat_axis=5, tiled=True),
        "lev",
        split_axis=3,
        concat_axis=4,
        tiled=True,
    )
    returned = returned.reshape(slot_count, 2, 2, fields // lev_count, half_lat)
    product = jnp.einsum(
        "skj,shrfj->shrfk",
        masked,
        lax.all_gather(returned, "lev", axis=3, tiled=True),
        preferred_element_type=jnp.float32,
    )
    return product[:, 0] + parity * product[:, 1]


def solution(mesh):
    return jax.shard_map(
        local,
        mesh=mesh,
        in_specs=(
            P("lat", None, None, "lev"),
            P("lat", "lev", None),
            P("lat", None, None),
            P(),
            P(),
            P(),
        ),
        out_specs=P("lat", None, None, "lev"),
        check_vma=False,
    )
```

profile of v0, /device:TPU:0, one launch (start us, length us, event | category | flops | bytes accessed | tf_op | source)
XLA Modules:
  0.0 1765.0 jit_solution(16773899357934970792)
XLA Ops:
  7.0 32.9 %all-reduce.2 = bf16[2,2,2,8,2560]{4,2,1,0,3:T(2,128)(2,1)} all-reduce(f32[2,2,2,8,2560]{4,2,1,0,3:T(2,128)} %copy.33), channel_id=2, replica_groups=mesh['lat'=4,'lev'=8] {'lev'}, use_global_device_ids=true, to_apply=%region_0.1.clone | all-reduce | flops 163840 | bytes 983040
  42.6 4.9 all-to-all-start
  47.5 5.7 all-to-all-done
  57.5 4.7 all-to-all-done.1
  64.0 1673.6 %while.14 = (s32[]{:T(128)}, bf16[80,8,2,2,8]{1,3,4,2,0:T(2,128)(2,1)}, bf16[80,8,2,2,8]{4,1,3,2,0:T(8,128)(2,1)}, s32[80]{0:T(128)S(1)}, s32[2560]{0:T(1024)}, ...) while((s32[]{:T(128)}, ...), condition=%wide.region_2.3_spmd.clone.clone, body=%wide.region_1.2_spmd.clone.clone.sunk | while | flops 17651100 | bytes 2342472 | solution.py:88
  76.5 4.4 fusion.57
  97.4 4.4 fusion.57
  118.3 4.4 fusion.57
  139.3 4.4 fusion.57
  160.2 4.4 fusion.57
  181.1 4.4 fusion.57
  202.0 4.4 fusion.57
  222.9 4.4 fusion.57
  243.8 4.4 fusion.57
  264.8 4.4 fusion.57
  285.7 4.4 fusion.57
  306.6 4.4 fusion.57
  327.5 4.4 fusion.57
  348.4 4.4 fusion.57
  369.4 4.4 fusion.57
  390.3 4.4 fusion.57
  411.2 4.4 fusion.57
  432.1 4.4 fusion.57
  453.0 4.4 fusion.57
  474.0 4.4 fusion.57
  494.9 4.4 fusion.57
  515.8 4.4 fusion.57
  536.7 4.4 fusion.57
  557.6 4.4 fusion.57
  1739.2 8.1 all_to_all.54
  1747.4 7.4 all_to_all.55
  1754.9 8.5 all_gather.3
  (1128 shorter events, 1218.3 us)
Async XLA Ops:
  1.9 3.0 copy-start.1
  4.9 34.9 %copy-start.4 = (u32[32]{0:T(128)S(1)}, u32[32]{0:T(128)}, u32[]{:S(2)}) copy-start(u32[32]{0:T(128)} %constant.110) | copy-start | bytes 388
  4.9 59.0 %copy-start.2 = (s32[8]{0:T(128)S(1)}, s32[8]{0:T(128)}, u32[]{:S(2)}) copy-start(s32[8]{0:T(128)} %param.11) | copy-start | bytes 100
  4.9 59.0 %copy-start.3 = (bf16[8,8]{1,0:T(8,128)(2,1)S(1)}, bf16[8,8]{1,0:T(8,128)(2,1)}, u32[]{:S(2)}) copy-start(bf16[8,8]{1,0:T(8,128)(2,1)} %param.13) | copy-start | bytes 388
  42.6 10.6 all-to-all-start
  53.9 8.3 all-to-all-start.1
  80.9 0.7 copy-start
  122.8 0.7 copy-start
  143.7 0.7 copy-start
  164.6 0.7 copy-start
  269.2 0.7 copy-start
  373.8 0.7 copy-start
  415.6 0.7 copy-start
  457.5 0.7 copy-start
  478.4 0.7 copy-start
  499.3 0.7 copy-start
  562.1 0.7 copy-start
  624.9 0.7 copy-start
  645.8 0.7 copy-start
  666.7 0.7 copy-start
  708.5 0.7 copy-start
  834.1 0.7 copy-start
  896.8 0.7 copy-start
  959.6 0.7 copy-start
  980.5 0.7 copy-start
  1022.4 0.7 copy-start
  1043.3 0.7 copy-start
  1085.1 0.7 copy-start
  1106.0 0.7 copy-start
  1189.7 0.7 copy-start
  1210.7 0.7 copy-start
  1378.0 0.7 copy-start
  (54 other events, 35.9 us)
where the time goes:
time: 1780 us; the launch traced here: 1770 us
  other arithmetic  763 us (43%)
  loops' own time  368 us (21%)
  local copies, waits for them, and re-layouts  350 us (20%)
  matrix products  208 us (12%)
  blocking collectives  56.9 us (3%)
    another operation x1, loops' own time, local(): analysed = lax.map(row_work, (jnp.moveaxis(fourier, 4, 0), row_ids))  368 us
    neg x80, other arithmetic, row_work(): phases_table = jnp.concatenate([cosine_table, -sine_table], axis=0)  355 us
    convert_element_type x80, other arithmetic, row_work(): cosine_table = jnp.where(inside, jnp.cos(angles), 0.0).astype(jnp.bfloat16)  354 us
    dot_general x80, matrix products, row_work(): lax.dot_general(column, phases_table, (((1,), (1,)), ((), ())), preferred...  126 us
    dynamic_slice x80, local copies, waits for them, and re-layouts, row_work(): length = circle_lengths[row_id]  107 us
    dot_general x80, matrix products, row_work(): jnp.dot(coeffs, phases_table, preferred_element_type=jnp.float32)  77.7 us
    transpose x160, local copies, waits for them, and re-layouts, row_work(): jnp.transpose(fourier_row, (1, 3, 2, 0)).reshape(2 * fields, 2 * wave_count)  63.5 us
    dynamic_update_slice x80, local copies, waits for them, and re-layouts, local(): analysed = lax.map(row_work, (jnp.moveaxis(fourier, 4, 0), row_ids))  52.9 us
  transfers between devices with their start and end apart: 2, of which 2 were waited for; matrix products, arithmetic and copies ran while one was open for 0% of the time, Pallas kernels for 0%

commit v1 on v0

v1 whole, which is shorter than its diff:
```python
import functools
import math

import jax
import jax.numpy as jnp
from jax import lax
from jax.experimental import pallas as pl
from jax.experimental.pallas import tpu as pltpu
from jax.sharding import PartitionSpec as P

BLK = 128
TILES = 4


def row_kernel(
    fields, lengths, values_ref, mixer_ref, keep_ref, fold_ref, signs_ref, table_ref, weight_ref,
    out_ref, left, total,
):
    rows, lanes = values_ref.shape
    hf = 2 * fields
    width = signs_ref.shape[1]
    waves = width // 2
    span = TILES * BLK
    values = values_ref[...]
    mixed = jnp.concatenate(
        [
            jnp.dot(values[:, at : at + BLK], mixer_ref[...], preferred_element_type=jnp.float32)
            for at in range(0, lanes, BLK)
        ],
        axis=1,
    )
    keep = keep_ref[...]
    scale = (2.0 * waves) ** (-0.5)
    for part, source in enumerate((values.astype(jnp.float32), mixed)):
        spread = (source[:, None, :] * keep[None, :, :]).reshape(rows * hf, lanes)
        folded = scale * jnp.dot(
            spread.astype(jnp.bfloat16), fold_ref[...], preferred_element_type=jnp.float32
        )
        for image in range(4):
            signed = folded * signs_ref[image : image + 1, :]
            at = (2 * image + part) * hf
            left[:, at : at + hf, :] = signed.reshape(rows, hf, width).astype(jnp.bfloat16)

    lane = lax.broadcasted_iota(jnp.int32, (1, span), 1)

    def row_body(row, carry):
        quarter = lengths[row] // 4
        coeffs = left[row]
        step_cos = table_ref[row, 2 * waves : 3 * waves, :]
        step_sin = table_ref[row, 3 * waves : 4 * waves, :]

        def chunk(index, state):
            cos_now, sin_now, sums = state
            cosines, sines = [], []
            for _ in range(TILES):
                cosines.append(cos_now)
                sines.append(-sin_now)
                cos_now, sin_now = (
                    cos_now * step_cos - sin_now * step_sin,
                    sin_now * step_cos + cos_now * step_sin,
                )
            phases = jnp.concatenate(
                [jnp.concatenate(cosines, axis=1), jnp.concatenate(sines, axis=1)], axis=0
            ).astype(jnp.bfloat16)
            grid = jnp.dot(coeffs, phases, preferred_element_type=jnp.float32)
            position = lane + index * span
            share = jnp.where(
                (position == 0) | (position == quarter),
                0.5,
                jnp.where(position < quarter, 1.0, 0.0),
            ).astype(jnp.float32)
            columns = []
            for image in range(4):
                at = 2 * image * hf
                columns.append(
                    ((grid[at : at + hf] + jnp.tanh(grid[at + hf : at + 2 * hf])) * share).astype(
                        jnp.bfloat16
                    )
                )
            sums = sums + lax.dot_general(
                jnp.concatenate(columns, axis=0),
                phases,
                (((1,), (1,)), ((), ())),
                preferred_element_type=jnp.float32,
            )
            return cos_now, sin_now, sums

        start = (
            table_ref[row, 0:waves, :],
            table_ref[row, waves : 2 * waves, :],
            jnp.zeros((4 * hf, width), jnp.float32),
        )
        _, _, sums = lax.fori_loop(0, quarter // span + 1, chunk, start)
        whole = sum(
            sums[image * hf : (image + 1) * hf] * signs_ref[image : image + 1, :]
            for image in range(4)
        )
        total[row] = whole * weight_ref[row]
        return carry

    lax.fori_loop(0, rows, row_body, 0)
    spread = lax.dot_general(
        total[...].reshape(rows * hf, width).astype(jnp.bfloat16),
        fold_ref[...],
        (((1,), (1,)), ((), ())),
        preferred_element_type=jnp.float32,
    )
    out_ref[...] = jnp.sum(spread.reshape(rows, hf, lanes) * keep[None, :, :], axis=1).astype(
        jnp.bfloat16
    )


def wave_tables(deal_list, lengths):
    rows, waves = lengths.shape[0], deal_list.shape[0]
    length = lengths.astype(jnp.float32)[:, None, None]
    wave = deal_list.astype(jnp.float32)[None, :, None]

    def angle_of(position):
        product = wave * position
        turned = product - jnp.floor(product / length) * length
        return turned * (2.0 * math.pi) / length

    inner = angle_of(jnp.arange(BLK, dtype=jnp.float32)[None, None, :])
    step = angle_of(jnp.full((1, 1, 1), float(BLK), jnp.float32))
    shape = (rows, waves, BLK)
    return jnp.concatenate(
        [
            jnp.cos(inner),
            jnp.sin(inner),
            jnp.broadcast_to(jnp.cos(step), shape),
            jnp.broadcast_to(jnp.sin(step), shape),
        ],
        axis=1,
    )


def rows_step(values, row_ids, deal_list, circle_lengths, mixing, slots, half_lat):
    rows, lanes = values.shape
    fields = mixing.shape[0]
    waves = deal_list.shape[0]
    hf, width = 2 * fields, 2 * waves
    lengths = circle_lengths[row_ids]
    tables = wave_tables(deal_list, lengths)
    weight = jnp.sin(math.pi * (row_ids.astype(jnp.float32) + 0.5) / (2 * half_lat)) / jnp.sqrt(
        lengths.astype(jnp.float32)
    )
    weight = jnp.broadcast_to(weight[:, None, None], (rows, 1, width))
    lane = jnp.arange(lanes, dtype=jnp.int32)
    lane_field = lane % fields
    lane_part = lane // fields % 2
    lane_half = lane // (2 * fields) % 2
    lane_wave = lane // (4 * fields)
    keep = (
        (lane_half * fields + lane_field)[None, :] == jnp.arange(hf, dtype=jnp.int32)[:, None]
    ).astype(jnp.float32)
    fold = (
        (lane_part * waves + lane_wave)[:, None] == jnp.arange(width, dtype=jnp.int32)[None, :]
    ).astype(jnp.bfloat16)
    parity = (1 - 2 * (deal_list % 2)).astype(jnp.float32)
    both = jnp.concatenate([parity, parity])
    flip = jnp.concatenate([jnp.ones_like(parity), -jnp.ones_like(parity)])
    signs = jnp.stack([jnp.ones_like(both), flip, both, both * flip])
    block = jnp.arange(BLK, dtype=jnp.int32)
    same = (block[:, None] // fields) == (block[None, :] // fields)
    mixer = jnp.where(
        same, jnp.tile(mixing.T, (BLK // fields, BLK // fields)), jnp.bfloat16(0)
    )
    vmem = pl.BlockSpec(memory_space=pltpu.VMEM)
    return pl.pallas_call(
        functools.partial(row_kernel, fields),
        out_shape=jax.ShapeDtypeStruct((rows, lanes), jnp.bfloat16),
        in_specs=[pl.BlockSpec(memory_space=pltpu.SMEM)] + [vmem] * 7,
        out_specs=vmem,
        scratch_shapes=[
            pltpu.VMEM((rows, 8 * hf, width), jnp.bfloat16),
            pltpu.VMEM((rows, hf, width), jnp.float32),
        ],
    )(lengths, values, mixer, keep, fold, signs, tables, weight)


def local(spec_in, legendre, pattern, deal_list, circle_lengths, mixing):
    lat_index = lax.axis_index("lat")
    lev_index = lax.axis_index("lev")
    lat_count = lax.axis_size("lat")
    lev_count = lax.axis_size("lev")
    slots, local_cols, half_lat = legendre.shape
    fields = spec_in.shape[2]
    devices = lat_count * lev_count
    rows = half_lat // devices
    span = 4 * slots * fields
    global_cols = lev_index * local_cols + jnp.arange(local_cols, dtype=jnp.int32)
    parity = (1 - 2 * (global_cols % 2)).astype(jnp.float32)
    col_live = pattern[:, -1, :][:, global_cols // BLK]
    row_live = jnp.repeat(pattern[:, :, 0], BLK, axis=1)
    kept = spec_in * col_live[:, None, None, :].astype(jnp.bfloat16)
    signed = (kept.astype(jnp.float32) * parity).astype(jnp.bfloat16)
    stacked = jnp.stack([kept, signed], axis=1)
    partial_value = jnp.einsum(
        "skj,shrfk->shrfj", legendre, stacked, preferred_element_type=jnp.float32
    )
    partial_value = partial_value * row_live[:, None, None, None, :].astype(jnp.float32)
    by_device = jnp.transpose(
        partial_value.reshape(span, rows, lev_count, lat_count), (2, 3, 1, 0)
    )
    summed = lax.psum_scatter(by_device, "lev", scatter_dimension=0, tiled=True).astype(
        jnp.bfloat16
    )
    fourier = lax.all_to_all(summed[0], "lat", split_axis=0, concat_axis=0, tiled=True)
    values = jnp.transpose(fourier, (1, 0, 2)).reshape(rows, lat_count * span)
    row_ids = (
        jnp.arange(rows, dtype=jnp.int32) * devices + lev_index * lat_count + lat_index
    )
    analysed = rows_step(values, row_ids, deal_list, circle_lengths, mixing, slots, half_lat)
    leaving = jnp.transpose(analysed.reshape(rows, lat_count, span), (1, 0, 2))
    returned = lax.all_to_all(leaving, "lat", split_axis=0, concat_axis=0, tiled=True)
    gathered = lax.all_gather(returned, "lev", axis=0, tiled=False)
    ordered = jnp.transpose(gathered, (3, 2, 0, 1)).reshape(slots, 2, 2, fields, half_lat)
    ordered = ordered * row_live[:, None, None, None, :].astype(jnp.bfloat16)
    product = jnp.einsum(
        "skj,shrfj->shrfk", legendre, ordered, preferred_element_type=jnp.float32
    )
    live = col_live[:, None, None, :].astype(jnp.float32)
    return (product[:, 0] + parity * product[:, 1]) * live


def solution(mesh):
    return jax.shard_map(
        local,
        mesh=mesh,
        in_specs=(
            P("lat", None, None, "lev"),
            P("lat", "lev", None),
            P("lat", None, None),
            P(),
            P(),
            P(),
        ),
        out_specs=P("lat", None, None, "lev"),
        check_vma=False,
    )
```

time: 1780 us -> 221 us (0.12)
  other arithmetic: 763 us -> 22.5 us
  loops' own time: 368 us -> 0 us
  local copies, waits for them, and re-layouts: 350 us -> 62.4 us
  matrix products: 208 us -> 4.35 us
  Pallas kernels: 0 us -> 63.5 us
  blocking collectives: 56.9 us -> 10.4 us
  waiting for transfers between devices: 10.5 us -> 35.6 us
    another operation x1 -> x0, loops' own time: 368 us -> none  [local(): analysed = lax.map(row_work, (jnp.moveaxis(fourier, 4, 0), row_ids))]
    neg x80 -> x0, other arithmetic: 355 us -> none  [row_work(): phases_table = jnp.concatenate([cosine_table, -sine_table], axis=0)]
    convert_element_type x81 -> x7, other arithmetic: 355 us -> 3.54 us  [the longest x1 1.02 us: local(): live = col_live[:, None, None, :].astype(jnp.float32)]
    dot_general x163 -> x2, matrix products: 208 us -> 4.35 us  [the longest x1 2.84 us: local(): jnp.einsum('skj,shrfj->shrfk', legendre, ordered, preferred_element_type=...]
    dynamic_slice x160 -> x0, local copies, waits for them, and re-layouts: 159 us -> none  [the longest x80 107 us: row_work(): length = circle_lengths[row_id]]
    pallas_call x0 -> x1, Pallas kernels: none -> 63.5 us  [rows_step(): pl.pallas_call(functools.partial(row_kernel, fields), out_shape=jax.Shape...]
    transpose x160 -> x2, local copies, waits for them, and re-layouts: 63.5 us -> 2.59 us  [the longest x1 2.51 us: local(): jnp.transpose(partial_value.reshape(span, rows, lev_count, lat_count), (2...]
    while x161 -> x0, local copies, waits for them, and re-layouts: 54.1 us -> none
  transfers between devices with their start and end apart: 2 -> 3, of which waited for: 2 -> 3; matrix products, arithmetic and copies ran while one was open for 0% -> 7% of each run, Pallas kernels for 0% -> 0%
where the time goes in v1:
time: 221 us; the launch traced here: 220 us
  Pallas kernels  63.5 us (29%)
  local copies, waits for them, and re-layouts  62.4 us (28%)
  waiting for transfers between devices  35.6 us (16%)
  other arithmetic  22.5 us (10%)
  between operations  13.6 us (6%)
  blocking collectives  10.4 us (5%)
  starting transfers between devices  7.89 us (4%)
  matrix products  4.35 us (2%)
    pallas_call x1, Pallas kernels, rows_step(): pl.pallas_call(functools.partial(row_kernel, fields), out_shape=jax.Shape...  63.5 us
    reduce_scatter x1, waiting for transfers between devices, local(): lax.psum_scatter(by_device, 'lev', scatter_dimension=0, tiled=True)  28.5 us
    reshape x1, local copies, waits for them, and re-layouts, local(): jnp.transpose(gathered, (3, 2, 0, 1)).reshape(slots, 2, 2, fields, half_lat)  16.8 us
    reshape x1, local copies, waits for them, and re-layouts, local(): partial_value.reshape(span, rows, lev_count, lat_count)  15.6 us
    mul x1, local copies, waits for them, and re-layouts, local(): partial_value * row_live[:, None, None, None, :].astype(jnp.float32)  11.4 us
    all_gather x1, blocking collectives, local(): gathered = lax.all_gather(returned, 'lev', axis=0, tiled=False)  10.4 us
    mul x1, other arithmetic, local(): ordered = ordered * row_live[:, None, None, None, :].astype(jnp.bfloat16)  9.09 us
    all_to_all x1, waiting for transfers between devices, local(): lax.all_to_all(leaving, 'lat', split_axis=0, concat_axis=0, tiled=True)  5.5 us
  transfers between devices with their start and end apart: 3, of which 3 were waited for; matrix products, arithmetic and copies ran while one was open for 7% of the time, Pallas kernels for 0%

profile of v1, /device:TPU:0, one launch (start us, length us, event | category | flops | bytes accessed | tf_op | source)
XLA Modules:
  0.0 220.3 jit_solution(16042480368236837100)
XLA Ops:
  7.2 1.0 slice_bitcast_fusion.2
  8.1 0.8 copy.73
  9.7 1.6 gather_fusion.1
  11.3 1.0 convert_bitcast_fusion
  12.4 0.8 multiply_bitcast_fusion
  13.2 0.8 fusion.17
  14.0 1.5 convolution_multiply_fusion
  15.5 11.4 %copy.54 = f32[2,2,2,8,2560]{3,2,1,0,4:T(2,128)} copy(f32[2,2,2,8,2560]{4,3,2,1,0:T(8,128)} %convolution_multiply_fusion) | data formatting | bytes 1310720 | tf_op jit(solution)/shard_map/mul | solution.py:201
  26.9 15.6 %reshape.486 = f32[64,80,8,4]{0,3,2,1:T(4,128)} reshape(f32[2,2,2,8,2560]{3,2,1,0,4:T(2,128)} %copy.54) | data formatting | bytes 1310720 | tf_op jit(solution)/shard_map/reshape | solution.py:203
  42.5 2.5 %copy.55 = f32[8,4,80,64]{2,3,1,0:T(8,128)} copy(f32[8,4,80,64]{3,1,0,2:T(4,128)} %bitcast.68) | data formatting | bytes 1310720 | tf_op jit(solution)/shard_map/transpose | solution.py:202
  45.2 1.1 gather_fusion
  46.5 0.9 tile.4
  47.4 1.5 tile.10
  51.9 0.7 fusion.10.fold_ref
  53.4 2.1 fusion.9
  55.5 28.5 %reduce-scatter.2.cloned.1.call-done = f32[1,4,80,64]{2,3,1,0:T(8,128)} async-done(((f32[8,4,80,64]{2,3,1,0:T(8,128)}), f32[1,4,80,64]{2,3,1,0:T(8,128)}) %reduce-scatter.2.cloned.1.call-update) | async-done | bytes 81936 | tf_op jit(solution)/shard_map/reduce_scatter | solution.py:205
  84.0 1.5 convert_bitcast_fusion.2
  85.5 4.6 %all-to-all-start = ((bf16[4,80,64]{1,2,0:T(8,128)(2,1)}), bf16[4,80,64]{1,2,0:T(8,128)(2,1)S(1)}, u32[]{:S(2)}, u32[]{:S(2)}) async-start(bf16[4,80,64]{1,2,0:T(8,128)(2,1)} %convert_bitcast_fusion.2), calls=%async_computation.1 | async-start | bytes 131072 | tf_op jit(solution)/shard_map/all_to_all | solution.py:208
  90.1 0.9 broadcast_in_dim.16
  91.0 0.9 broadcast_in_dim.15
  92.0 2.2 %pad_maximum_fusion.table_ref = f32[80,32,128]{2,1,0:T(8,128)} fusion(f32[80,8,128]{2,1,0:T(8,128)S(1)} %broadcast_in_dim.16, f32[80,8,128]{2,1,0:T(8,128)S(1)} %broadcast_in_dim.15, f32[80,8,128]{2,1,0:T(8,128)} %get-tuple-element.8, f32[80,8,128]{2,1,0:T(8,128)} %get-tuple-element.7), kind=kLoop, calls=%fused_computation.8 | loop fusion | flops 983040 | bytes 2621440 | tf_op jit(solution)/shard_map/concatenate | solution.py:126
  94.2 1.7 all-to-all-done
  96.6 0.8 broadcast_in_dim.17.weight_ref
  97.3 63.5 %shard_map.64 = bf16[80,256]{1,0:T(8,128)(2,1)} custom-call(s32[80]{0:T(128)} %copy-done.3, bf16[80,256]{1,0:T(8,128)(2,1)} %copy.59.values_ref, bf16[128,128]{1,0:T(8,128)(2,1)} %compare_select_fusion.mixer_ref, f32[16,256]{1,0:T(8,128)} %fusion.18.keep_ref, bf16[256,16]{1,0:T(8,128)(2,1)} %fusion.10.fold_ref, f32[4,16]{1,0:T(4,128)} %pad_maximum_fusion.1.signs_ref, ...), custom_call_target="tpu_custom_call" | custom-call | tf_op jit(solution)/shard_map/pallas_call | solution.py:169
  160.8 1.5 copy.60
  162.3 3.3 %all-to-all-start.1 = ((bf16[4,80,64]{1,2,0:T(8,128)(2,1)}), bf16[4,80,64]{1,2,0:T(8,128)(2,1)S(1)}, u32[]{:S(2)}, u32[]{:S(2)}) async-start(bf16[4,80,64]{1,2,0:T(8,128)(2,1)} %bitcast.74), calls=%async_computation.2 | async-start | bytes 131072 | tf_op jit(solution)/shard_map/all_to_all | solution.py:215
  165.8 5.5 %all-to-all-done.1 = bf16[4,80,64]{1,2,0:T(8,128)(2,1)S(1)} async-done(((bf16[4,80,64]{1,2,0:T(8,128)(2,1)}), bf16[4,80,64]{1,2,0:T(8,128)(2,1)S(1)}, u32[]{:S(2)}, u32[]{:S(2)}) %all-to-all-start.1) | async-done | bytes 40992 | tf_op jit(solution)/shard_map/all_to_all | solution.py:215
  171.3 10.4 %all-gather = bf16[32,80,64]{1,2,0:T(8,128)(2,1)} all-gather(bf16[4,80,64]{1,2,0:T(8,128)(2,1)S(1)} %all-to-all-done.1), channel_id=2, replica_groups=mesh['lat'=4,'lev'=8] {'lev'}, dimensions={0}, use_global_device_ids=true | all-gather | bytes 368640 | tf_op jit(solution)/shard_map/all_gather | solution.py:216
  181.8 2.3 %copy.61 = bf16[8,4,80,64]{3,1,0,2:T(4,128)(2,1)} copy(bf16[8,4,80,64]{2,3,1,0:T(8,128)(2,1)} %bitcast.71) | data formatting | bytes 655360 | tf_op jit(solution)/shard_map/all_gather | solution.py:216
  184.0 16.8 %reshape.489 = bf16[2,2,2,8,2560]{3,2,1,0,4:T(2,128)(2,1)} reshape(bf16[64,80,8,4]{0,3,2,1:T(4,128)(2,1)} %bitcast.70) | data formatting | bytes 655360 | tf_op jit(solution)/shard_map/reshape | solution.py:217
  200.9 9.1 %broadcast_multiply_fusion = bf16[2,2,2,8,2560]{3,2,1,0,4:T(2,128)(2,1)S(1)} fusion(bf16[2,2,2,8,2560]{3,2,1,0,4:T(2,128)(2,1)} %reshape.489, bf16[2,2560]{0,1:T(8,128)(2,1)S(1)} %bitcast.69), kind=kLoop, calls=%fused_computation.7 | loop fusion | flops 163840 | bytes 665600 | tf_op jit(solution)/shard_map/mul | solution.py:218
  210.0 2.8 %fusion = f32[2,2,2,8,320]{4,3,2,0,1:T(8,128)S(1)} fusion(bf16[2,2,2,8,2560]{3,2,1,0,4:T(2,128)(2,1)S(1)} %broadcast_multiply_fusion, bf16[2,320,2560]{2,1,0:T(8,128)(2,1)S(1)} %copy-done), kind=kOutput, calls=%fused_computation.2 | convolution fusion | flops 104857600 | bytes 3686400 | tf_op jit(solution)/shard_map/skj,shrfj->shrfk/dot_general | solution.py:219
  (51 shorter events, 7.0 us)
Async XLA Ops:
  6.5 7.4 %copy-start = (bf16[2,320,2560]{2,1,0:T(8,128)(2,1)S(1)}, bf16[2,320,2560]{2,1,0:T(8,128)(2,1)}, u32[]{:S(2)}) copy-start(bf16[2,320,2560]{2,1,0:T(8,128)(2,1)} %param.7) | copy-start | bytes 9830404
  6.5 77.4 %reduce-scatter.2.cloned.1.call-start = ((), (), s32[]{:S(2)}) async-start(), calls=%async_computation.3 | async-start | bytes 1179648 | tf_op jit(solution)/shard_map/reduce_scatter | solution.py:205
  42.5 2.6 %copy-start.7 = (s32[8]{0:T(128)S(1)}, s32[8]{0:T(128)}, u32[]{:S(2)}) copy-start(s32[8]{0:T(128)} %param.9) | copy-start | bytes 100
  42.5 2.6 %copy-start.1 = (s32[2560]{0:T(1024)S(1)}, s32[2560]{0:T(1024)}, u32[]{:S(2)}) copy-start(s32[2560]{0:T(1024)} %param.10) | copy-start | bytes 30724
  42.5 3.9 %copy-start.4 = (bf16[8,8]{1,0:T(8,128)(2,1)S(1)}, bf16[8,8]{1,0:T(8,128)(2,1)}, u32[]{:S(2)}) copy-start(bf16[8,8]{1,0:T(8,128)(2,1)} %param.11) | copy-start | bytes 388
  42.5 8.1 %copy-start.6 = (f32[1,16]{1,0:T(1,128)S(1)}, f32[1,16]{1,0:T(1,128)}, u32[]{:S(2)}) copy-start(f32[1,16]{1,0:T(1,128)} %constant.167.clone.1) | copy-start | bytes 196
  46.3 51.0 %copy-start.3 = (s32[80]{0:T(128)}, s32[80]{0:T(128)S(1)}, u32[]{:S(2)}) copy-start(s32[80]{0:T(128)S(1)} %gather_fusion) | copy-start | bytes 964
  49.1 116.5 %copy-start.5 = (bf16[2,20]{1,0:T(2,128)(2,1)S(1)}, bf16[2,20]{1,0:T(2,128)(2,1)}, u32[]{:S(2)}) copy-start(bf16[2,20]{1,0:T(2,128)(2,1)} %get-tuple-element.9) | copy-start | bytes 244
  85.5 10.4 %all-to-all-start = ((bf16[4,80,64]{1,2,0:T(8,128)(2,1)}), bf16[4,80,64]{1,2,0:T(8,128)(2,1)S(1)}, u32[]{:S(2)}, u32[]{:S(2)}) async-start(bf16[4,80,64]{1,2,0:T(8,128)(2,1)} %convert_bitcast_fusion.2), calls=%async_computation.1 | async-start | bytes 131072 | tf_op jit(solution)/shard_map/all_to_all | solution.py:208
  162.3 9.0 %all-to-all-start.1 = ((bf16[4,80,64]{1,2,0:T(8,128)(2,1)}), bf16[4,80,64]{1,2,0:T(8,128)(2,1)S(1)}, u32[]{:S(2)}, u32[]{:S(2)}) async-start(bf16[4,80,64]{1,2,0:T(8,128)(2,1)} %bitcast.74), calls=%async_computation.2 | async-start | bytes 131072 | tf_op jit(solution)/shard_map/all_to_all | solution.py:215
  210.0 2.9 %copy-start.2 = (f32[320]{0:T(512)S(1)}, f32[320]{0:T(512)}, u32[]{:S(2)}) copy-start(f32[320]{0:T(512)} %fusion.26) | copy-start | bytes 3844
Sparse Core Ops, SparseCore 0:
  45.2 38.7 reduce-scatter.1

commit v2 on v1

--- a/solution.py
+++ b/solution.py
@@ -13,7 +13,7 @@
 
 
 def row_kernel(
-    fields, lengths, values_ref, mixer_ref, keep_ref, fold_ref, signs_ref, table_ref, weight_ref,
+    fields, lengths, values_ref, live_ref, mixer_ref, keep_ref, fold_ref, signs_ref, table_ref, weight_ref,
     out_ref, left, total,
 ):
     rows, lanes = values_ref.shape
@@ -21,7 +21,8 @@
     width = signs_ref.shape[1]
     waves = width // 2
     span = TILES * BLK
-    values = values_ref[...]
+    live = live_ref[...]
+    values = values_ref[...] * live
     mixed = jnp.concatenate(
         [
             jnp.dot(values[:, at : at + BLK], mixer_ref[...], preferred_element_type=jnp.float32)
@@ -105,9 +106,8 @@
         (((1,), (1,)), ((), ())),
         preferred_element_type=jnp.float32,
     )
-    out_ref[...] = jnp.sum(spread.reshape(rows, hf, lanes) * keep[None, :, :], axis=1).astype(
-        jnp.bfloat16
-    )
+    summed = jnp.sum(spread.reshape(rows, hf, lanes) * keep[None, :, :], axis=1)
+    out_ref[...] = summed.astype(jnp.bfloat16) * live
 
 
 def wave_tables(deal_list, lengths):
@@ -150,6 +150,9 @@
     lane_part = lane // fields % 2
     lane_half = lane // (2 * fields) % 2
     lane_wave = lane // (4 * fields)
+    first_live = (deal_list * (half_lat // BLK)) // (2 * half_lat)
+    first_lane = jnp.repeat(first_live, lanes // waves)
+    live = (row_ids[:, None] // BLK >= first_lane[None, :]).astype(jnp.bfloat16)
     keep = (
         (lane_half * fields + lane_field)[None, :] == jnp.arange(hf, dtype=jnp.int32)[:, None]
     ).astype(jnp.float32)
@@ -169,13 +172,130 @@
     return pl.pallas_call(
         functools.partial(row_kernel, fields),
         out_shape=jax.ShapeDtypeStruct((rows, lanes), jnp.bfloat16),
-        in_specs=[pl.BlockSpec(memory_space=pltpu.SMEM)] + [vmem] * 7,
+        in_specs=[pl.BlockSpec(memory_space=pltpu.SMEM)] + [vmem] * 8,
         out_specs=vmem,
         scratch_shapes=[
             pltpu.VMEM((rows, 8 * hf, width), jnp.bfloat16),
             pltpu.VMEM((rows, hf, width), jnp.float32),
         ],
-    )(lengths, values, mixer, keep, fold, signs, tables, weight)
+    )(lengths, values, live, mixer, keep, fold, signs, tables, weight)
+
+
+def peers_of(axis):
+    count = lax.axis_size(axis)
+    return [lax.rem(lax.axis_index(axis) + off, count) for off in range(1, count)]
+
+
+def greet():
+    barrier = pltpu.get_barrier_semaphore()
+    total = 0
+    for axis in ("lat", "lev"):
+        for peer in peers_of(axis):
+            pl.semaphore_signal(
+                barrier, inc=1, device_id={axis: peer}, device_id_type=pl.DeviceIdType.MESH
+            )
+            total += 1
+    pl.semaphore_wait(barrier, total)
+
+
+def send(axis, sources, target, sems):
+    copies = []
+    for step, peer in enumerate(peers_of(axis)):
+        copy = pltpu.make_async_remote_copy(
+            src_ref=sources(peer),
+            dst_ref=target,
+            send_sem=sems.at[0, step],
+            recv_sem=sems.at[1, step],
+            device_id={axis: peer},
+            device_id_type=pl.DeviceIdType.MESH,
+        )
+        copy.start()
+        copies.append(copy)
+    return copies
+
+
+def inward_kernel(pack, spec_ref, legendre_ref, out_ref, turned, leaving, arriving, summed, landed,
+                  lev_sems, lat_sems):
+    slots, _, half_lat = legendre_ref.shape
+    lev_count, lat_count, count, width = leaving.shape
+    devices = lev_count * lat_count
+    lev_index, lat_index = lax.axis_index("lev"), lax.axis_index("lat")
+    packed = half_lat // pack
+    sums = [
+        jnp.dot(spec_ref[slot], legendre_ref[slot], preferred_element_type=jnp.float32)
+        for slot in range(slots)
+    ]
+    for block in range(packed // BLK):
+        piece = jnp.concatenate(
+            [
+                value[:, part * packed + block * BLK : part * packed + (block + 1) * BLK]
+                for part in range(pack)
+                for value in sums
+            ],
+            axis=0,
+        )
+        turned[:, block * BLK : (block + 1) * BLK, :] = jnp.stack(
+            [piece[at : at + BLK].T for at in range(0, width, BLK)]
+        )
+    for device in range(devices):
+        for at in range(width // BLK):
+            leaving[device // lat_count, device % lat_count, :, at * BLK : (at + 1) * BLK] = (
+                turned[at, pl.ds(device, count, stride=devices), :].astype(jnp.bfloat16)
+            )
+    greet()
+    copies = send("lev", lambda peer: leaving.at[peer], arriving.at[lev_index], lev_sems)
+    total = leaving[lev_index].astype(jnp.float32)
+    for copy, peer in zip(copies, [lax.rem(lev_index + lev_count - off, lev_count) for off in range(1, lev_count)]):
+        copy.wait_recv()
+        total = total + arriving[peer].astype(jnp.float32)
+    summed[...] = total.astype(jnp.bfloat16)
+    crossing = send("lat", lambda peer: summed.at[peer], landed.at[lat_index], lat_sems)
+    out_ref[lat_index] = summed[lat_index]
+    for copy, peer in zip(crossing, [lax.rem(lat_index + lat_count - off, lat_count) for off in range(1, lat_count)]):
+        copy.wait_recv()
+        out_ref[peer] = landed[peer]
+    for copy in copies + crossing:
+        copy.wait_send()
+
+
+def outward_kernel(pack, fields, rows_ref, legendre_ref, out_ref, held, landed, gathered, turned,
+                   lev_sems, lat_sems, load_sem):
+    slots, local_cols, half_lat = held.shape
+    lev_count, lat_count, count, width = gathered.shape
+    devices = lev_count * lat_count
+    lev_index, lat_index = lax.axis_index("lev"), lax.axis_index("lat")
+    packed = half_lat // pack
+    part_width = 4 * fields
+    load = pltpu.make_async_copy(legendre_ref, held, load_sem)
+    load.start()
+    greet()
+    crossing = send("lat", lambda peer: rows_ref.at[peer], landed.at[lat_index], lat_sems)
+    landed[lat_index] = rows_ref[lat_index]
+    for copy in crossing:
+        copy.wait_recv()
+    copies = send("lev", lambda peer: landed, gathered.at[lev_index], lev_sems)
+    gathered[lev_index] = landed[...]
+    for copy in copies:
+        copy.wait_recv()
+    for device in range(devices):
+        block = gathered[device // lat_count, device % lat_count].astype(jnp.float32)
+        for at in range(width // BLK):
+            turned[at, pl.ds(device, count, stride=devices), :] = block[:, at * BLK : (at + 1) * BLK]
+    load.wait()
+    sides = [turned[at].astype(jnp.bfloat16) for at in range(width // BLK)]
+    for slot in range(slots):
+        total = None
+        for part in range(pack):
+            at = part * slots * part_width + slot * part_width
+            value = jnp.dot(
+                held[slot, :, part * packed : (part + 1) * packed],
+                sides[at // BLK],
+                preferred_element_type=jnp.float32,
+            )[:, at % BLK : at % BLK + part_width]
+            total = value if total is None else total + value
+        out_ref[slot] = total
+    for copy in copies + crossing:
+        copy.wait_send()
 
 
 def local(spec_in, legendre, pattern, deal_list, circle_lengths, mixing):
@@ -188,39 +308,74 @@
     devices = lat_count * lev_count
     rows = half_lat // devices
     span = 4 * slots * fields
+    pack = max(1, BLK // span)
+    count, width = rows // pack, span * pack
     global_cols = lev_index * local_cols + jnp.arange(local_cols, dtype=jnp.int32)
     parity = (1 - 2 * (global_cols % 2)).astype(jnp.float32)
-    col_live = pattern[:, -1, :][:, global_cols // BLK]
-    row_live = jnp.repeat(pattern[:, :, 0], BLK, axis=1)
-    kept = spec_in * col_live[:, None, None, :].astype(jnp.bfloat16)
-    signed = (kept.astype(jnp.float32) * parity).astype(jnp.bfloat16)
-    stacked = jnp.stack([kept, signed], axis=1)
-    partial_value = jnp.einsum(
-        "skj,shrfk->shrfj", legendre, stacked, preferred_element_type=jnp.float32
-    )
-    partial_value = partial_value * row_live[:, None, None, None, :].astype(jnp.float32)
-    by_device = jnp.transpose(
-        partial_value.reshape(span, rows, lev_count, lat_count), (2, 3, 1, 0)
-    )
-    summed = lax.psum_scatter(by_device, "lev", scatter_dimension=0, tiled=True).astype(
-        jnp.bfloat16
-    )
-    fourier = lax.all_to_all(summed[0], "lat", split_axis=0, concat_axis=0, tiled=True)
-    values = jnp.transpose(fourier, (1, 0, 2)).reshape(rows, lat_count * span)
+    chooser = (
+        global_cols[None, :] // BLK
+        == jnp.arange(pattern.shape[2], dtype=jnp.int32)[:, None]
+    )
+    col_live = jnp.sum(
+        jnp.where(chooser[None], pattern[:, -1, :, None], 0), axis=1
+    ).astype(jnp.float32)
+    kept = spec_in.astype(jnp.float32) * col_live[:, None, None, :]
+    stacked = (
+        jnp.stack([kept, kept * parity], axis=1)
+        .astype(jnp.bfloat16)
+        .reshape(slots, 4 * fields, local_cols)
+    )
+    vmem = pl.BlockSpec(memory_space=pltpu.VMEM)
+    block_shape = (lat_count, count, width)
+    sems = [
+        pltpu.SemaphoreType.DMA((2, lev_count)),
+        pltpu.SemaphoreType.DMA((2, lat_count)),
+    ]
+    turned = pltpu.VMEM((width // BLK, half_lat // pack, BLK), jnp.float32)
+    fourier = pl.pallas_call(
+        functools.partial(inward_kernel, pack),
+        out_shape=jax.ShapeDtypeStruct(block_shape, jnp.bfloat16),
+        in_specs=[vmem, vmem],
+        out_specs=vmem,
+        scratch_shapes=[
+            turned,
+            pltpu.VMEM((lev_count,) + block_shape, jnp.bfloat16),
+            pltpu.VMEM((lev_count,) + block_shape, jnp.bfloat16),
+            pltpu.VMEM(block_shape, jnp.bfloat16),
+            pltpu.VMEM(block_shape, jnp.bfloat16),
+        ]
+        + sems,
+        compiler_params=pltpu.CompilerParams(collective_id=0, has_side_effects=True),
+    )(stacked, legendre)
+    values = jnp.transpose(
+        fourier.reshape(lat_count, count, pack, span), (2, 1, 0, 3)
+    ).reshape(rows, lat_count * span)
     row_ids = (
-        jnp.arange(rows, dtype=jnp.int32) * devices + lev_index * lat_count + lat_index
-    )
+        jnp.arange(pack, dtype=jnp.int32)[:, None] * (half_lat // pack)
+        + jnp.arange(count, dtype=jnp.int32)[None, :] * devices
+        + (lev_index * lat_count + lat_index)
+    ).reshape(rows)
     analysed = rows_step(values, row_ids, deal_list, circle_lengths, mixing, slots, half_lat)
-    leaving = jnp.transpose(analysed.reshape(rows, lat_count, span), (1, 0, 2))
-    returned = lax.all_to_all(leaving, "lat", split_axis=0, concat_axis=0, tiled=True)
-    gathered = lax.all_gather(returned, "lev", axis=0, tiled=False)
-    ordered = jnp.transpose(gathered, (3, 2, 0, 1)).reshape(slots, 2, 2, fields, half_lat)
-    ordered = ordered * row_live[:, None, None, None, :].astype(jnp.bfloat16)
-    product = jnp.einsum(
-        "skj,shrfj->shrfk", legendre, ordered, preferred_element_type=jnp.float32
-    )
-    live = col_live[:, None, None, :].astype(jnp.float32)
-    return (product[:, 0] + parity * product[:, 1]) * live
+    leaving = jnp.transpose(
+        analysed.reshape(pack, count, lat_count, span), (2, 1, 0, 3)
+    ).reshape(block_shape)
+    product = pl.pallas_call(
+        functools.partial(outward_kernel, pack, fields),
+        out_shape=jax.ShapeDtypeStruct((slots, local_cols, 4 * fields), jnp.float32),
+        in_specs=[vmem, pl.BlockSpec(memory_space=pl.ANY)],
+        out_specs=vmem,
+        scratch_shapes=[
+            pltpu.VMEM(legendre.shape, jnp.bfloat16),
+            pltpu.VMEM(block_shape, jnp.bfloat16),
+            pltpu.VMEM((lev_count,) + block_shape, jnp.bfloat16),
+            turned,
+        ]
+        + sems
+        + [pltpu.SemaphoreType.DMA],
+        compiler_params=pltpu.CompilerParams(collective_id=1, has_side_effects=True),
+    )(leaving, legendre)
+    product = jnp.transpose(product, (0, 2, 1)).reshape(slots, 2, 2, fields, local_cols)
+    return (product[:, 0] + parity * product[:, 1]) * col_live[:, None, None, :]
 
 
 def solution(mesh):

time: 221 us -> 111 us (0.50)
  local copies, waits for them, and re-layouts: 62.4 us -> 9.76 us
  waiting for transfers between devices: 35.6 us -> 0 us
  Pallas kernels: 63.5 us -> 92.3 us
  other arithmetic: 22.5 us -> 8.53 us
  between operations: 13.6 us -> 0.18 us
  blocking collectives: 10.4 us -> 0 us
  starting transfers between devices: 7.89 us -> 0 us
  matrix products: 4.35 us -> 0 us
    pallas_call x0 -> x2, Pallas kernels: none -> 31.7 us  [the longest x1 17.7 us: local(): pl.pallas_call(functools.partial(inward_kernel, pack), out_shape=jax.Shap...]
    reshape x3 -> x6, local copies, waits for them, and re-layouts: 33.1 us -> 3.31 us  [the longest x2 0.95 us: local(): analysed.reshape(pack, count, lat_count, span)]
    reduce_scatter x1 -> x0, waiting for transfers between devices: 28.5 us -> none  [local(): lax.psum_scatter(by_device, 'lev', scatter_dimension=0, tiled=True)]
    mul x1 -> x0, local copies, waits for them, and re-layouts: 11.4 us -> none  [local(): partial_value * row_live[:, None, None, None, :].astype(jnp.float32)]
    all_gather x1 -> x0, blocking collectives: 10.4 us -> none  [local(): gathered = lax.all_gather(returned, 'lev', axis=0, tiled=False)]
    mul x2 -> x3, other arithmetic: 9.74 us -> 0.65 us  [the longest x1 0.64 us: local(): return (product[:, 0] + parity * product[:, 1]) * col_live[:, None, None, :]]
    all_to_all x2 -> x0, starting transfers between devices: 7.89 us -> none  [the longest x1 4.61 us: local(): lax.all_to_all(summed[0], 'lat', split_axis=0, concat_axis=0, tiled=True)]
    all_to_all x2 -> x0, waiting for transfers between devices: 7.16 us -> none  [the longest x1 5.5 us: local(): lax.all_to_all(leaving, 'lat', split_axis=0, concat_axis=0, tiled=True)]
  transfers between devices with their start and end apart: 3 -> 0, of which waited for: 3 -> 0; matrix products, arithmetic and copies ran while one was open for 7% -> 0% of each run, Pallas kernels for 0% -> 0%
where the time goes in v2:
time: 111 us
  Pallas kernels  92.3 us (83%)
  local copies, waits for them, and re-layouts  9.76 us (9%)
  other arithmetic  8.53 us (8%)
    pallas_call x1, Pallas kernels, rows_step(): pl.pallas_call(functools.partial(row_kernel, fields), out_shape=jax.Shape...  60.7 us
    pallas_call x1, Pallas kernels, local(): pl.pallas_call(functools.partial(inward_kernel, pack), out_shape=jax.Shap...  17.7 us
    pallas_call x1, Pallas kernels, local(): pl.pallas_call(functools.partial(outward_kernel, pack, fields), out_shape...  14 us

profile of v2, /device:TPU:0, one launch (start us, length us, event | category | flops | bytes accessed | tf_op | source)
XLA Modules:
  0.0 110.8 jit_solution(9380944115776922618)
XLA Ops:
  0.2 0.5 copy-done
  0.7 1.1 %gather_fusion = s32[80]{0:T(128)S(1)} fusion(s32[2560]{0:T(1024)S(1)} %copy-done, s32[1024]{0:T(1024)S(1)} %pad_clamp_fusion), kind=kCustom, calls=%fused_computation | custom fusion | bytes 960 | tf_op jit(solution)/shard_map/gather | solution.py:142
  1.9 0.7 fusion.40
  2.7 1.3 %fusion.5 = (f32[80,8,128]{2,1,0:T(8,128)S(1)}, f32[80,8,128]{2,1,0:T(8,128)S(1)}) fusion(f32[80]{0:T(128)S(1)} %convert_element_type.63, f32[8,128]{1,0:T(8,128)S(1)} %iota_multiply_fusion), kind=kLoop, calls=%fused_computation.8 | loop fusion | flops 491520 | bytes 659776 | tf_op jit(solution)/shard_map/cos | solution.py:128
  4.0 0.7 broadcast_multiply_fusion
  4.6 0.1 fusion.23
  4.8 0.1 copy.30
  4.9 0.1 broadcast_in_dim.39
  5.0 0.1 copy.31
  5.1 0.1 broadcast_in_dim.40
  5.3 1.2 %pad_maximum_fusion.table_ref = f32[80,32,128]{2,1,0:T(8,128)} fusion(f32[80,8,128]{2,1,0:T(8,128)S(1)} %broadcast_in_dim.40, f32[80,8,128]{2,1,0:T(8,128)S(1)} %broadcast_in_dim.39, f32[80,8,128]{2,1,0:T(8,128)S(1)} %get-tuple-element.8, f32[80,8,128]{2,1,0:T(8,128)S(1)} %get-tuple-element.7), kind=kLoop, calls=%fused_computation.1 | loop fusion | flops 983040 | bytes 2621440 | tf_op jit(solution)/shard_map/concatenate | solution.py:126
  6.5 0.7 slice_bitcast_fusion.2
  7.1 0.1 copy.26
  7.2 0.1 select_reduce_fusion
  7.4 0.6 copy.27
  8.0 17.7 %shard_map.64 = bf16[4,40,128]{2,1,0:T(8,128)(2,1)} custom-call(bf16[2,32,320]{2,1,0:T(8,128)(2,1)} %bitcast.42, bf16[2,320,2560]{2,1,0:T(8,128)(2,1)} %legendre_ref.3), custom_call_target="tpu_custom_call" | custom-call | tf_op jit(solution)/shard_map/pallas_call | solution.py:335
  25.8 0.9 reshape.568
  26.7 0.7 reshape.569.values_ref
  27.5 0.8 broadcast_in_dim.41.weight_ref
  28.5 0.7 compare_convert_fusion.live_ref
  29.3 0.6 pad_maximum_fusion.2.signs_ref
  30.1 0.1 tile.4
  30.2 0.5 tile.10
  30.7 0.7 compare_select_fusion.mixer_ref
  31.4 0.7 fusion.6.fold_ref
  32.1 0.6 fusion.13.keep_ref
  32.7 60.7 %shard_map.65 = bf16[80,256]{1,0:T(8,128)(2,1)} custom-call(s32[80]{0:T(128)} %copy-done.3, bf16[80,256]{1,0:T(8,128)(2,1)} %reshape.569.values_ref, bf16[80,256]{1,0:T(8,128)(2,1)} %compare_convert_fusion.live_ref, bf16[128,128]{1,0:T(8,128)(2,1)} %compare_select_fusion.mixer_ref, f32[16,256]{1,0:T(8,128)} %fusion.13.keep_ref, ...), custom_call_target="tpu_custom_call" | custom-call | tf_op jit(solution)/shard_map/pallas_call | solution.py:172
  93.4 0.9 reshape.570
  94.4 0.7 reshape.571.rows_ref
  95.1 14.0 %shard_map.66 = f32[2,320,32]{2,1,0:T(8,128)} custom-call(bf16[4,40,128]{2,1,0:T(8,128)(2,1)} %reshape.571.rows_ref, bf16[2,320,2560]{2,1,0:T(8,128)(2,1)} %legendre_ref.3), custom_call_target="tpu_custom_call" | custom-call | tf_op jit(solution)/shard_map/pallas_call | solution.py:362
  109.1 1.1 copy.33
  110.2 0.6 fusion.9
  (36 shorter events, 1.0 us)
Async XLA Ops:
  0.0 0.7 copy-start
  1.9 25.6 %copy-start.3 = (s32[80]{0:T(128)}, s32[80]{0:T(128)S(1)}, u32[]{:S(2)}) copy-start(s32[80]{0:T(128)S(1)} %gather_fusion) | copy-start | bytes 964
  5.2 2.1 %copy-start.1 = (bf16[2,2,8,320]{3,2,1,0:T(8,128)(2,1)S(1)}, bf16[2,2,8,320]{3,2,1,0:T(8,128)(2,1)}, u32[]{:S(2)}) copy-start(bf16[2,2,8,320]{3,2,1,0:T(8,128)(2,1)} %param.6) | copy-start | bytes 61444
  8.0 21.2 %copy-start.4 = (f32[1,16]{1,0:T(1,128)S(1)}, f32[1,16]{1,0:T(1,128)}, u32[]{:S(2)}) copy-start(f32[1,16]{1,0:T(1,128)} %constant.186.clone.1) | copy-start | bytes 196
  8.0 21.9 %copy-start.2 = (bf16[8,8]{1,0:T(8,128)(2,1)S(1)}, bf16[8,8]{1,0:T(8,128)(2,1)}, u32[]{:S(2)}) copy-start(bf16[8,8]{1,0:T(8,128)(2,1)} %param.11) | copy-start | bytes 388

commit v3 on v2

--- a/solution.py
+++ b/solution.py
@@ -9,7 +9,8 @@
 from jax.sharding import PartitionSpec as P
 
 BLK = 128
-TILES = 4
+TILES = 2
+STREAMS = 8
 
 
 def row_kernel(
@@ -32,26 +33,42 @@
     )
     keep = keep_ref[...]
     scale = (2.0 * waves) ** (-0.5)
-    for part, source in enumerate((values.astype(jnp.float32), mixed)):
+
+    def fold(source):
         spread = (source[:, None, :] * keep[None, :, :]).reshape(rows * hf, lanes)
-        folded = scale * jnp.dot(
+        return scale * jnp.dot(
             spread.astype(jnp.bfloat16), fold_ref[...], preferred_element_type=jnp.float32
         )
+
+    high = mixed.astype(jnp.bfloat16).astype(jnp.float32)
+    straight, mix_high, mix_low = fold(values.astype(jnp.float32)), fold(high), fold(mixed - high)
+    pairs = (
+        jnp.concatenate([straight, jnp.zeros_like(straight)], axis=1),
+        jnp.concatenate([mix_high, mix_low], axis=1),
+    )
+    for part, source in enumerate(pairs):
         for image in range(4):
-            signed = folded * signs_ref[image : image + 1, :]
+            sign = signs_ref[image : image + 1, :]
+            signed = source * jnp.concatenate([sign, sign], axis=1)
             at = (2 * image + part) * hf
-            left[:, at : at + hf, :] = signed.reshape(rows, hf, width).astype(jnp.bfloat16)
+            left[:rows, at : at + hf, :] = signed.reshape(rows, hf, 2 * width).astype(jnp.bfloat16)
 
     lane = lax.broadcasted_iota(jnp.int32, (1, span), 1)
 
-    def row_body(row, carry):
-        quarter = lengths[row] // 4
-        coeffs = left[row]
-        step_cos = table_ref[row, 2 * waves : 3 * waves, :]
-        step_sin = table_ref[row, 3 * waves : 4 * waves, :]
-
-        def chunk(index, state):
-            cos_now, sin_now, sums = state
+    def proceed(state):
+        return state[1]
+
+    def advance(state):
+        following, _, streams = state
+        stages = []
+        for row, index, cos_held, sin_held, sums in streams:
+            quarter = lengths[jnp.minimum(row, rows - 1)] // 4
+            at = jnp.minimum(row, rows - 1)
+            fresh = index == 0
+            cos_now = jnp.where(fresh, table_ref[at, 0:waves, :], cos_held)
+            sin_now = jnp.where(fresh, table_ref[at, waves : 2 * waves, :], sin_held)
+            step_cos = table_ref[at, 2 * waves : 3 * waves, :]
+            step_sin = table_ref[at, 3 * waves : 4 * waves, :]
             cosines, sines = [], []
             for _ in range(TILES):
                 cosines.append(cos_now)
@@ -63,8 +80,19 @@
             phases = jnp.concatenate(
                 [jnp.concatenate(cosines, axis=1), jnp.concatenate(sines, axis=1)], axis=0
             ).astype(jnp.bfloat16)
-            grid = jnp.dot(coeffs, phases, preferred_element_type=jnp.float32)
-            position = lane + index * span
+            stages.append((at, quarter, fresh, cos_now, sin_now, phases))
+        grids = [
+            jnp.dot(
+                left[stage[0]],
+                jnp.concatenate([stage[5], stage[5]], axis=0),
+                preferred_element_type=jnp.float32,
+            )
+            for stage in stages
+        ]
+        added = []
+        for stream, stage, grid in zip(streams, stages, grids):
+            quarter, phases = stage[1], stage[5]
+            position = lane + stream[1] * span
             share = jnp.where(
                 (position == 0) | (position == quarter),
                 0.5,
@@ -78,30 +106,51 @@
                         jnp.bfloat16
                     )
                 )
-            sums = sums + lax.dot_general(
-                jnp.concatenate(columns, axis=0),
-                phases,
-                (((1,), (1,)), ((), ())),
-                preferred_element_type=jnp.float32,
-            )
-            return cos_now, sin_now, sums
-
-        start = (
-            table_ref[row, 0:waves, :],
-            table_ref[row, waves : 2 * waves, :],
+            added.append(
+                lax.dot_general(
+                    jnp.concatenate(columns, axis=0),
+                    phases,
+                    (((1,), (1,)), ((), ())),
+                    preferred_element_type=jnp.float32,
+                )
+            )
+        later = []
+        busy = jnp.bool_(False)
+        for stream, stage, extra in zip(streams, stages, added):
+            row, index, _, _, sums = stream
+            sums = jnp.where(stage[2], 0.0, sums) + extra
+            whole = sum(
+                sums[image * hf : (image + 1) * hf] * signs_ref[image : image + 1, :]
+                for image in range(4)
+            )
+            total[row] = whole * weight_ref[stage[0]]
+            done = (index + 1) * span > stage[1]
+            idle = row >= rows
+            taken = jnp.logical_and(done, jnp.logical_not(idle))
+            row = jnp.where(taken, following, row)
+            following = following - taken.astype(jnp.int32)
+            row = jnp.where(row < 0, rows, row)
+            index = jnp.where(done, 0, index + 1)
+            busy = jnp.logical_or(busy, row < rows)
+            later.append((row, index, stage[3], stage[4], sums))
+        return following, busy, tuple(later)
+
+    held = jnp.zeros((waves, BLK), jnp.float32)
+    streams = tuple(
+        (
+            jnp.int32(rows - 1 - stream if stream < rows else rows),
+            jnp.int32(0),
+            held,
+            held,
             jnp.zeros((4 * hf, width), jnp.float32),
         )
-        _, _, sums = lax.fori_loop(0, quarter // span + 1, chunk, start)
-        whole = sum(
-            sums[image * hf : (image + 1) * hf] * signs_ref[image : image + 1, :]
-            for image in range(4)
-        )
-        total[row] = whole * weight_ref[row]
-        return carry
-
-    lax.fori_loop(0, rows, row_body, 0)
+        for stream in range(STREAMS)
+    )
+    lax.while_loop(
+        proceed, advance, (jnp.int32(rows - 1 - STREAMS), jnp.bool_(True), streams)
+    )
     spread = lax.dot_general(
-        total[...].reshape(rows * hf, width).astype(jnp.bfloat16),
+        total[:rows].reshape(rows * hf, width).astype(jnp.bfloat16),
         fold_ref[...],
         (((1,), (1,)), ((), ())),
         preferred_element_type=jnp.float32,
@@ -175,8 +224,8 @@
         in_specs=[pl.BlockSpec(memory_space=pltpu.SMEM)] + [vmem] * 8,
         out_specs=vmem,
         scratch_shapes=[
-            pltpu.VMEM((rows, 8 * hf, width), jnp.bfloat16),
-            pltpu.VMEM((rows, hf, width), jnp.float32),
+            pltpu.VMEM((rows, 8 * hf, 2 * width), jnp.bfloat16),
+            pltpu.VMEM((rows + 1, hf, width), jnp.float32),
         ],
     )(lengths, values, live, mixer, keep, fold, signs, tables, weight)
 
@@ -244,7 +293,19 @@
             )
     greet()
     copies = send("lev", lambda peer: leaving.at[peer], arriving.at[lev_index], lev_sems)
-    total = leaving[lev_index].astype(jnp.float32)
+    mine = lev_index * lat_count
+    total = jnp.stack(
+        [
+            jnp.concatenate(
+                [
+                    turned[at, pl.ds(mine + side, count, stride=devices), :]
+                    for at in range(width // BLK)
+                ],
+                axis=1,
+            )
+            for side in range(lat_count)
+        ]
+    )
     for copy, peer in zip(copies, [lax.rem(lev_index + lev_count - off, lev_count) for off in range(1, lev_count)]):
         copy.wait_recv()
         total = total + arriving[peer].astype(jnp.float32)

time: 111 us -> 71.8 us (0.65)
  Pallas kernels: 92.3 us -> 52.7 us
    pallas_call x1, Pallas kernels: 60.7 us -> 21.7 us  [rows_step(): pl.pallas_call(functools.partial(row_kernel, fields), out_shape=jax.Shape...]
where the time goes in v3:
time: 71.8 us; the launch traced here: 71.2 us
  Pallas kernels  52.7 us (73%)
  local copies, waits for them, and re-layouts  9.76 us (14%)
  other arithmetic  8.53 us (12%)
    pallas_call x1, Pallas kernels, rows_step(): pl.pallas_call(functools.partial(row_kernel, fields), out_shape=jax.Shape...  21.7 us
    pallas_call x1, Pallas kernels, local(): pl.pallas_call(functools.partial(inward_kernel, pack), out_shape=jax.Shap...  17.7 us
    pallas_call x1, Pallas kernels, local(): pl.pallas_call(functools.partial(outward_kernel, pack, fields), out_shape...  13.3 us

profile of v3, /device:TPU:0, one launch (start us, length us, event | category | flops | bytes accessed | tf_op | source)
XLA Modules:
  0.0 71.2 jit_solution(6364907770808905378)
XLA Ops:
  0.2 0.5 copy-done
  0.7 1.1 %gather_fusion = s32[80]{0:T(128)S(1)} fusion(s32[2560]{0:T(1024)S(1)} %copy-done, s32[1024]{0:T(1024)S(1)} %pad_clamp_fusion), kind=kCustom, calls=%fused_computation | custom fusion | bytes 960 | tf_op jit(solution)/shard_map/gather | solution.py:191
  1.9 0.7 %fusion.40 = (f32[8]{0:T(128)S(1)}, s32[8]{0:T(128)S(1)}, f32[8]{0:T(128)S(1)}) fusion(s32[8]{0:T(128)} %param.9), kind=kLoop, calls=%fused_computation.106 | loop fusion | flops 192 | bytes 128 | tf_op jit(solution)/shard_map/convert_element_type | solution.py:165
  2.7 1.3 %fusion.5 = (f32[80,8,128]{2,1,0:T(8,128)S(1)}, f32[80,8,128]{2,1,0:T(8,128)S(1)}) fusion(f32[80]{0:T(128)S(1)} %convert_element_type.63, f32[8,128]{1,0:T(8,128)S(1)} %iota_multiply_fusion), kind=kLoop, calls=%fused_computation.8 | loop fusion | flops 491520 | bytes 659776 | tf_op jit(solution)/shard_map/cos | solution.py:177
  4.0 0.7 broadcast_multiply_fusion
  4.6 0.1 fusion.23
  4.8 0.1 copy.30
  4.9 0.1 broadcast_in_dim.39
  5.0 0.1 copy.31
  5.1 0.1 broadcast_in_dim.40
  5.3 1.2 %pad_maximum_fusion.table_ref = f32[80,32,128]{2,1,0:T(8,128)} fusion(f32[80,8,128]{2,1,0:T(8,128)S(1)} %broadcast_in_dim.40, f32[80,8,128]{2,1,0:T(8,128)S(1)} %broadcast_in_dim.39, f32[80,8,128]{2,1,0:T(8,128)S(1)} %get-tuple-element.8, f32[80,8,128]{2,1,0:T(8,128)S(1)} %get-tuple-element.7), kind=kLoop, calls=%fused_computation.1 | loop fusion | flops 983040 | bytes 2621440 | tf_op jit(solution)/shard_map/concatenate | solution.py:175
  6.5 0.7 slice_bitcast_fusion.2
  7.1 0.1 copy.26
  7.2 0.1 select_reduce_fusion
  7.4 0.6 copy.27
  8.0 17.7 %shard_map.64 = bf16[4,40,128]{2,1,0:T(8,128)(2,1)} custom-call(bf16[2,32,320]{2,1,0:T(8,128)(2,1)} %bitcast.42, bf16[2,320,2560]{2,1,0:T(8,128)(2,1)} %legendre_ref.3), custom_call_target="tpu_custom_call" | custom-call | tf_op jit(solution)/shard_map/pallas_call | solution.py:396
  25.8 0.9 %reshape.568 = bf16[4,40,2,64]{3,2,1,0:T(2,128)(2,1)S(1)} reshape(bf16[4,40,128]{2,1,0:T(8,128)(2,1)} %shard_map.64) | data formatting | bytes 81920 | tf_op jit(solution)/shard_map/reshape | solution.py:412
  26.7 0.7 %reshape.569.values_ref = bf16[80,256]{1,0:T(8,128)(2,1)} reshape(bf16[2,40,4,64]{3,2,1,0:T(4,128)(2,1)S(1)} %bitcast.40) | data formatting | bytes 81920 | tf_op jit(solution)/shard_map/reshape | solution.py:413
  27.5 0.8 %broadcast_in_dim.41.weight_ref = f32[80,1,16]{2,1,0:T(1,128)} broadcast(f32[80]{0:T(128)S(1)} %rsqrt_multiply_fusion), dimensions={0} | broadcast | bytes 5440 | tf_op jit(solution)/shard_map/broadcast_in_dim | solution.py:196
  28.5 0.7 compare_convert_fusion.live_ref
  29.3 0.6 pad_maximum_fusion.2.signs_ref
  30.1 0.1 tile.4
  30.2 0.5 tile.10
  30.7 0.7 compare_select_fusion.mixer_ref
  31.4 0.7 %fusion.6.fold_ref = bf16[256,16]{1,0:T(8,128)(2,1)} fusion(s32[256]{0:T(256)S(1)} %fusion.31), kind=kLoop, calls=%fused_computation.10 | loop fusion | flops 8192 | bytes 9216 | tf_op jit(solution)/shard_map/convert_element_type | solution.py:210
  32.1 0.6 fusion.13.keep_ref
  32.7 21.7 %shard_map.65 = bf16[80,256]{1,0:T(8,128)(2,1)} custom-call(s32[80]{0:T(128)} %copy-done.3, bf16[80,256]{1,0:T(8,128)(2,1)} %reshape.569.values_ref, bf16[80,256]{1,0:T(8,128)(2,1)} %compare_convert_fusion.live_ref, bf16[128,128]{1,0:T(8,128)(2,1)} %compare_select_fusion.mixer_ref, f32[16,256]{1,0:T(8,128)} %fusion.13.keep_ref, ...), custom_call_target="tpu_custom_call" | custom-call | tf_op jit(solution)/shard_map/pallas_call | solution.py:221
  54.4 0.9 %reshape.570 = bf16[2,40,4,64]{3,2,1,0:T(4,128)(2,1)S(1)} reshape(bf16[80,256]{1,0:T(8,128)(2,1)} %shard_map.65) | data formatting | bytes 81920 | tf_op jit(solution)/shard_map/reshape | solution.py:421
  55.4 0.7 %reshape.571.rows_ref = bf16[4,40,128]{2,1,0:T(8,128)(2,1)} reshape(bf16[4,40,2,64]{3,2,1,0:T(2,128)(2,1)S(1)} %bitcast.41) | data formatting | bytes 81920 | tf_op jit(solution)/shard_map/reshape | solution.py:422
  56.1 13.3 %shard_map.66 = f32[2,320,32]{2,1,0:T(8,128)} custom-call(bf16[4,40,128]{2,1,0:T(8,128)(2,1)} %reshape.571.rows_ref, bf16[2,320,2560]{2,1,0:T(8,128)(2,1)} %legendre_ref.3), custom_call_target="tpu_custom_call" | custom-call | tf_op jit(solution)/shard_map/pallas_call | solution.py:423
  69.4 1.1 %copy.33 = f32[2,32,320]{2,1,0:T(8,128)S(1)} copy(f32[2,32,320]{1,2,0:T(8,128)} %bitcast.38) | data formatting | bytes 163840 | tf_op jit(solution)/shard_map/transpose | solution.py:438
  70.5 0.6 fusion.9
  (36 shorter events, 1.0 us)
Async XLA Ops:
  0.0 0.7 copy-start
  1.9 25.6 %copy-start.3 = (s32[80]{0:T(128)}, s32[80]{0:T(128)S(1)}, u32[]{:S(2)}) copy-start(s32[80]{0:T(128)S(1)} %gather_fusion) | copy-start | bytes 964
  5.2 2.1 %copy-start.1 = (bf16[2,2,8,320]{3,2,1,0:T(8,128)(2,1)S(1)}, bf16[2,2,8,320]{3,2,1,0:T(8,128)(2,1)}, u32[]{:S(2)}) copy-start(bf16[2,2,8,320]{3,2,1,0:T(8,128)(2,1)} %param.6) | copy-start | bytes 61444
  8.0 21.2 %copy-start.4 = (f32[1,16]{1,0:T(1,128)S(1)}, f32[1,16]{1,0:T(1,128)}, u32[]{:S(2)}) copy-start(f32[1,16]{1,0:T(1,128)} %constant.186.clone.1) | copy-start | bytes 196
  8.0 21.9 %copy-start.2 = (bf16[8,8]{1,0:T(8,128)(2,1)S(1)}, bf16[8,8]{1,0:T(8,128)(2,1)}, u32[]{:S(2)}) copy-start(bf16[8,8]{1,0:T(8,128)(2,1)} %param.11) | copy-start | bytes 388

commit v4 on v3

--- a/solution.py
+++ b/solution.py
@@ -10,34 +10,89 @@
 
 BLK = 128
 TILES = 2
-STREAMS = 8
+STREAMS = 12
 
 
 def row_kernel(
-    fields, lengths, values_ref, live_ref, mixer_ref, keep_ref, fold_ref, signs_ref, table_ref, weight_ref,
-    out_ref, left, total,
+    packed, lengths, deal, fourier_ref, mixing_ref, table_ref, weight_ref, out_ref, left, total
 ):
-    rows, lanes = values_ref.shape
-    hf = 2 * fields
-    width = signs_ref.shape[1]
-    waves = width // 2
+    lat_count, count, block_width = fourier_ref.shape
+    rows = table_ref.shape[0]
+    waves = table_ref.shape[1] // 4
+    fields = mixing_ref.shape[0]
+    hf, width = 2 * fields, 2 * waves
+    pack = rows // count
+    part_span = block_width // pack
+    lanes = lat_count * part_span
     span = TILES * BLK
-    live = live_ref[...]
-    values = values_ref[...] * live
+    devices = lat_count * lax.axis_size("lev")
+    device = lax.axis_index("lev") * lat_count + lax.axis_index("lat")
+    lane_of = lax.broadcasted_iota(jnp.int32, (1, lanes), 1)
+    first_lane = jnp.zeros((1, lanes), jnp.int32)
+    kind = lax.broadcasted_iota(jnp.int32, (1, width), 1)
+    both = jnp.zeros((1, width), jnp.float32)
+    for wave in range(waves):
+        cut = deal[wave] * (pack * packed // BLK) // (2 * pack * packed)
+        first_lane = jnp.where(lane_of // (4 * fields) == wave, cut, first_lane)
+        odd = (1 - 2 * (deal[wave] % 2)).astype(jnp.float32)
+        both = jnp.where(kind % waves == wave, odd, both)
+    flip = jnp.where(kind < waves, 1.0, -1.0).astype(jnp.float32)
+    signs = [jnp.ones_like(both), flip, both, both * flip]
+    blocks = [fourier_ref[side].astype(jnp.float32) for side in range(lat_count)]
+    values = jnp.concatenate(
+        [
+            jnp.concatenate(
+                [block[:, part * part_span : (part + 1) * part_span] for block in blocks], axis=1
+            )
+            for part in range(pack)
+        ],
+        axis=0,
+    )
+    row_in = lax.broadcasted_iota(jnp.int32, (count, 1), 0) * devices + device
+    live = jnp.concatenate(
+        [
+            jnp.where((row_in + part * packed) // BLK >= first_lane, 1.0, 0.0)
+            for part in range(pack)
+        ],
+        axis=0,
+    ).astype(jnp.float32)
+    values = (values * live).astype(jnp.bfloat16)
+    keep_lane = lane_of // (2 * fields) % 2 * fields + lane_of % fields
+    keep = (
+        lax.broadcasted_iota(jnp.int32, (hf, lanes), 0) == keep_lane
+    ).astype(jnp.float32)
+    down = lax.broadcasted_iota(jnp.int32, (lanes, width), 0)
+    gather = (
+        down // fields % 2 * waves + down // (4 * fields)
+        == lax.broadcasted_iota(jnp.int32, (lanes, width), 1)
+    ).astype(jnp.float32).astype(jnp.bfloat16)
+    pick = (
+        lax.broadcasted_iota(jnp.int32, (BLK, fields), 0) % fields
+        == lax.broadcasted_iota(jnp.int32, (BLK, fields), 1)
+    ).astype(jnp.float32).astype(jnp.bfloat16)
+    across = (((1,), (1,)), ((), ()))
+    half_mixer = lax.dot_general(
+        pick, mixing_ref[...], across, preferred_element_type=jnp.float32
+    ).astype(jnp.bfloat16)
+    mixer = lax.dot_general(half_mixer, pick, across, preferred_element_type=jnp.float32)
+    same = (
+        lax.broadcasted_iota(jnp.int32, (BLK, BLK), 0) // fields
+        == lax.broadcasted_iota(jnp.int32, (BLK, BLK), 1) // fields
+    )
+    mixer = jnp.where(same, mixer, 0.0).astype(jnp.bfloat16)
     mixed = jnp.concatenate(
         [
-            jnp.dot(values[:, at : at + BLK], mixer_ref[...], preferred_element_type=jnp.float32)
+            jnp.dot(values[:, at : at + BLK], mixer, preferred_element_type=jnp.float32)
             for at in range(0, lanes, BLK)
         ],
         axis=1,
     )
-    keep = keep_ref[...]
     scale = (2.0 * waves) ** (-0.5)
 
     def fold(source):
         spread = (source[:, None, :] * keep[None, :, :]).reshape(rows * hf, lanes)
         return scale * jnp.dot(
-            spread.astype(jnp.bfloat16), fold_ref[...], preferred_element_type=jnp.float32
+            spread.astype(jnp.bfloat16), gather, preferred_element_type=jnp.float32
         )
 
     high = mixed.astype(jnp.bfloat16).astype(jnp.float32)
@@ -48,7 +103,7 @@
     )
     for part, source in enumerate(pairs):
         for image in range(4):
-            sign = signs_ref[image : image + 1, :]
+            sign = signs[image]
             signed = source * jnp.concatenate([sign, sign], axis=1)
             at = (2 * image + part) * hf
             left[:rows, at : at + hf, :] = signed.reshape(rows, hf, 2 * width).astype(jnp.bfloat16)
@@ -120,10 +175,10 @@
             row, index, _, _, sums = stream
             sums = jnp.where(stage[2], 0.0, sums) + extra
             whole = sum(
-                sums[image * hf : (image + 1) * hf] * signs_ref[image : image + 1, :]
+                sums[image * hf : (image + 1) * hf] * signs[image]
                 for image in range(4)
             )
-            total[row] = whole * weight_ref[stage[0]]
+            total[row] = whole
             done = (index + 1) * span > stage[1]
             idle = row >= rows
             taken = jnp.logical_and(done, jnp.logical_not(idle))
@@ -150,13 +205,23 @@
         proceed, advance, (jnp.int32(rows - 1 - STREAMS), jnp.bool_(True), streams)
     )
     spread = lax.dot_general(
-        total[:rows].reshape(rows * hf, width).astype(jnp.bfloat16),
-        fold_ref[...],
+        (total[:rows] * weight_ref[...]).reshape(rows * hf, width).astype(jnp.bfloat16),
+        gather,
         (((1,), (1,)), ((), ())),
         preferred_element_type=jnp.float32,
     )
     summed = jnp.sum(spread.reshape(rows, hf, lanes) * keep[None, :, :], axis=1)
-    out_ref[...] = summed.astype(jnp.bfloat16) * live
+    summed = summed * live
+    for side in range(lat_count):
+        out_ref[side] = jnp.concatenate(
+            [
+                summed[
+                    part * count : (part + 1) * count, side * part_span : (side + 1) * part_span
+                ]
+                for part in range(pack)
+            ],
+            axis=1,
+        ).astype(jnp.bfloat16)
 
 
 def wave_tables(deal_list, lengths):
@@ -183,51 +248,41 @@
     )
 
 
-def rows_step(values, row_ids, deal_list, circle_lengths, mixing, slots, half_lat):
-    rows, lanes = values.shape
-    fields = mixing.shape[0]
-    waves = deal_list.shape[0]
+def rows_step(fourier, lengths, row_ids, deal_list, mixing, half_lat):
+    fields, waves, rows = mixing.shape[0], deal_list.shape[0], row_ids.shape[0]
     hf, width = 2 * fields, 2 * waves
-    lengths = circle_lengths[row_ids]
+    pack = rows // fourier.shape[1]
     tables = wave_tables(deal_list, lengths)
     weight = jnp.sin(math.pi * (row_ids.astype(jnp.float32) + 0.5) / (2 * half_lat)) / jnp.sqrt(
         lengths.astype(jnp.float32)
     )
-    weight = jnp.broadcast_to(weight[:, None, None], (rows, 1, width))
-    lane = jnp.arange(lanes, dtype=jnp.int32)
-    lane_field = lane % fields
-    lane_part = lane // fields % 2
-    lane_half = lane // (2 * fields) % 2
-    lane_wave = lane // (4 * fields)
-    first_live = (deal_list * (half_lat // BLK)) // (2 * half_lat)
-    first_lane = jnp.repeat(first_live, lanes // waves)
-    live = (row_ids[:, None] // BLK >= first_lane[None, :]).astype(jnp.bfloat16)
-    keep = (
-        (lane_half * fields + lane_field)[None, :] == jnp.arange(hf, dtype=jnp.int32)[:, None]
-    ).astype(jnp.float32)
-    fold = (
-        (lane_part * waves + lane_wave)[:, None] == jnp.arange(width, dtype=jnp.int32)[None, :]
-    ).astype(jnp.bfloat16)
-    parity = (1 - 2 * (deal_list % 2)).astype(jnp.float32)
-    both = jnp.concatenate([parity, parity])
-    flip = jnp.concatenate([jnp.ones_like(parity), -jnp.ones_like(parity)])
-    signs = jnp.stack([jnp.ones_like(both), flip, both, both * flip])
-    block = jnp.arange(BLK, dtype=jnp.int32)
-    same = (block[:, None] // fields) == (block[None, :] // fields)
-    mixer = jnp.where(
-        same, jnp.tile(mixing.T, (BLK // fields, BLK // fields)), jnp.bfloat16(0)
-    )
     vmem = pl.BlockSpec(memory_space=pltpu.VMEM)
+    smem = pl.BlockSpec(memory_space=pltpu.SMEM)
     return pl.pallas_call(
-        functools.partial(row_kernel, fields),
-        out_shape=jax.ShapeDtypeStruct((rows, lanes), jnp.bfloat16),
-        in_specs=[pl.BlockSpec(memory_space=pltpu.SMEM)] + [vmem] * 8,
+        functools.partial(row_kernel, half_lat // pack),
+        out_shape=jax.ShapeDtypeStruct(fourier.shape, jnp.bfloat16),
+        in_specs=[smem, smem] + [vmem] * 4,
         out_specs=vmem,
         scratch_shapes=[
             pltpu.VMEM((rows, 8 * hf, 2 * width), jnp.bfloat16),
             pltpu.VMEM((rows + 1, hf, width), jnp.float32),
         ],
-    )(lengths, values, live, mixer, keep, fold, signs, tables, weight)
+    )(lengths, deal_list, fourier, mixing, tables, weight[:, None, None])
+
+
+def column_masks(pattern_ref, local_cols):
+    slots, blocks_down, blocks = pattern_ref.shape
+    column = lax.broadcasted_iota(jnp.int32, (1, local_cols), 1)
+    column = column + lax.axis_index("lev") * local_cols
+    odd = (1 - 2 * (column % 2)).astype(jnp.float32)
+    masks = []
+    for slot in range(slots):
+        mask = jnp.zeros((1, local_cols), jnp.float32)
+        for block in range(blocks):
+            kept = pattern_ref[slot, blocks_down - 1, block].astype(jnp.float32)
+            mask = jnp.where(column // BLK == block, kept, mask)
+        masks.append(mask)
+    return odd, masks
 
 
 def peers_of(axis):
@@ -263,17 +318,25 @@
     return copies
 
 
-def inward_kernel(pack, spec_ref, legendre_ref, out_ref, turned, leaving, arriving, summed, landed,
+def inward_kernel(pack, pattern_ref, spec_ref, legendre_ref, out_ref, turned, leaving, arriving, summed, landed,
                   lev_sems, lat_sems):
     slots, _, half_lat = legendre_ref.shape
     lev_count, lat_count, count, width = leaving.shape
     devices = lev_count * lat_count
     lev_index, lat_index = lax.axis_index("lev"), lax.axis_index("lat")
     packed = half_lat // pack
-    sums = [
-        jnp.dot(spec_ref[slot], legendre_ref[slot], preferred_element_type=jnp.float32)
-        for slot in range(slots)
-    ]
+    odd, masks = column_masks(pattern_ref, legendre_ref.shape[1])
+    sums = []
+    for slot in range(slots):
+        kept = jnp.concatenate([spec_ref[slot, 0], spec_ref[slot, 1]], axis=0).astype(jnp.float32)
+        kept = kept * masks[slot]
+        sums.append(
+            jnp.dot(
+                jnp.concatenate([kept, kept * odd], axis=0).astype(jnp.bfloat16),
+                legendre_ref[slot],
+                preferred_element_type=jnp.float32,
+            )
+        )
     for block in range(packed // BLK):
         piece = jnp.concatenate(
             [
@@ -319,7 +382,7 @@
         copy.wait_send()
 
 
-def outward_kernel(pack, fields, rows_ref, legendre_ref, out_ref, held, landed, gathered, turned,
+def outward_kernel(pack, fields, pattern_ref, rows_ref, legendre_ref, out_ref, held, landed, gathered, turned,
                    lev_sems, lat_sems, load_sem):
     slots, local_cols, half_lat = held.shape
     lev_count, lat_count, count, width = gathered.shape
@@ -343,6 +406,7 @@
         for at in range(width // BLK):
             turned[at, pl.ds(device, count, stride=devices), :] = block[:, at * BLK : (at + 1) * BLK]
     load.wait()
+    odd, masks = column_masks(pattern_ref, local_cols)
     sides = [turned[at].astype(jnp.bfloat16) for at in range(width // BLK)]
     for slot in range(slots):
         total = None
@@ -354,7 +418,9 @@
                 preferred_element_type=jnp.float32,
             )[:, at % BLK : at % BLK + part_width]
             total = value if total is None else total + value
-        out_ref[slot] = total
+        flat = total.T
+        joined = flat[: 2 * fields] + odd * flat[2 * fields :]
+        out_ref[slot] = joined * masks[slot]
     for copy in copies + crossing:
         copy.wait_send()
 
@@ -371,21 +437,6 @@
     span = 4 * slots * fields
     pack = max(1, BLK // span)
     count, width = rows // pack, span * pack
-    global_cols = lev_index * local_cols + jnp.arange(local_cols, dtype=jnp.int32)
-    parity = (1 - 2 * (global_cols % 2)).astype(jnp.float32)
-    chooser = (
-        global_cols[None, :] // BLK
-        == jnp.arange(pattern.shape[2], dtype=jnp.int32)[:, None]
-    )
-    col_live = jnp.sum(
-        jnp.where(chooser[None], pattern[:, -1, :, None], 0), axis=1
-    ).astype(jnp.float32)
-    kept = spec_in.astype(jnp.float32) * col_live[:, None, None, :]
-    stacked = (
-        jnp.stack([kept, kept * parity], axis=1)
-        .astype(jnp.bfloat16)
-        .reshape(slots, 4 * fields, local_cols)
-    )
     vmem = pl.BlockSpec(memory_space=pltpu.VMEM)
     block_shape = (lat_count, count, width)
     sems = [
@@ -396,7 +447,7 @@
     fourier = pl.pallas_call(
         functools.partial(inward_kernel, pack),
         out_shape=jax.ShapeDtypeStruct(block_shape, jnp.bfloat16),
-        in_specs=[vmem, vmem],
+        in_specs=[pl.BlockSpec(memory_space=pltpu.SMEM), vmem, vmem],
         out_specs=vmem,
         scratch_shapes=[
             turned,
@@ -407,23 +458,24 @@
         ]
         + sems,
         compiler_params=pltpu.CompilerParams(collective_id=0, has_side_effects=True),
-    )(stacked, legendre)
-    values = jnp.transpose(
-        fourier.reshape(lat_count, count, pack, span), (2, 1, 0, 3)
-    ).reshape(rows, lat_count * span)
+    )(pattern, spec_in, legendre)
     row_ids = (
         jnp.arange(pack, dtype=jnp.int32)[:, None] * (half_lat // pack)
         + jnp.arange(count, dtype=jnp.int32)[None, :] * devices
         + (lev_index * lat_count + lat_index)
     ).reshape(rows)
-    analysed = rows_step(values, row_ids, deal_list, circle_lengths, mixing, slots, half_lat)
-    leaving = jnp.transpose(
-        analysed.reshape(pack, count, lat_count, span), (2, 1, 0, 3)
-    ).reshape(block_shape)
+    by_device = circle_lengths.reshape(rows, devices)
+    chosen = jnp.arange(devices, dtype=jnp.int32)[None, :] == lev_index * lat_count + lat_index
+    lengths = jnp.sum(jnp.where(chosen, by_device, 0), axis=1)
+    leaving = rows_step(fourier, lengths, row_ids, deal_list, mixing, half_lat)
     product = pl.pallas_call(
         functools.partial(outward_kernel, pack, fields),
-        out_shape=jax.ShapeDtypeStruct((slots, local_cols, 4 * fields), jnp.float32),
-        in_specs=[vmem, pl.BlockSpec(memory_space=pl.ANY)],
+        out_shape=jax.ShapeDtypeStruct((slots, 2 * fields, local_cols), jnp.float32),
+        in_specs=[
+            pl.BlockSpec(memory_space=pltpu.SMEM),
+            vmem,
+            pl.BlockSpec(memory_space=pl.ANY),
+        ],
         out_specs=vmem,
         scratch_shapes=[
             pltpu.VMEM(legendre.shape, jnp.bfloat16),
@@ -434,9 +486,8 @@
         + sems
         + [pltpu.SemaphoreType.DMA],
         compiler_params=pltpu.CompilerParams(collective_id=1, has_side_effects=True),
-    )(leaving, legendre)
-    product = jnp.transpose(product, (0, 2, 1)).reshape(slots, 2, 2, fields, local_cols)
-    return (product[:, 0] + parity * product[:, 1]) * col_live[:, None, None, :]
+    )(pattern, leaving, legendre)
+    return product.reshape(slots, 2, fields, local_cols)
 
 
 def solution(mesh):

time: 71.8 us -> 58.8 us (0.82)
  local copies, waits for them, and re-layouts: 9.76 us -> 4.09 us
  other arithmetic: 8.53 us -> 4.18 us
  Pallas kernels: 52.7 us -> 49.9 us
    pallas_call x1, Pallas kernels: 21.7 us -> 18.5 us  [rows_step(): pl.pallas_call(functools.partial(row_kernel, half_lat // pack), out_shape...]
    reshape x6 -> x1, local copies, waits for them, and re-layouts: 3.31 us -> 0.78 us  [local(): by_device = circle_lengths.reshape(rows, devices)]
    convert_element_type x4 -> x0, other arithmetic: 2.03 us -> none  [the longest x1 0.72 us: rows_step(): fold = ((lane_part * waves + lane_wave)[:, None] == jnp.arange(width, dty...]
    broadcast_in_dim x4 -> x0, local copies, waits for them, and re-layouts: 1.62 us -> none  [the longest x2 0.78 us: local(): jnp.where(chooser[None], pattern[:, -1, :, None], 0)]
    unnamed x10 -> x6, local copies, waits for them, and re-layouts: 0.54 us -> 2.03 us
    another operation x4 -> x0, local copies, waits for them, and re-layouts: 1.25 us -> none  [the longest x1 0.63 us: local(): jnp.stack([kept, kept * parity], axis=1).astype(jnp.bfloat16)]
    transpose x2 -> x0, local copies, waits for them, and re-layouts: 1.19 us -> none  [the longest x1 1.11 us: local(): jnp.transpose(product, (0, 2, 1)).reshape(slots, 2, 2, fields, local_cols)]
    gather x1 -> x0, local copies, waits for them, and re-layouts: 1.15 us -> none  [rows_step(): lengths = circle_lengths[row_ids]]
where the time goes in v4:
time: 58.8 us; the launch traced here: 58.3 us
  Pallas kernels  49.9 us (85%)
  other arithmetic  4.18 us (7%)
  local copies, waits for them, and re-layouts  4.09 us (7%)
    pallas_call x1, Pallas kernels, rows_step(): pl.pallas_call(functools.partial(row_kernel, half_lat // pack), out_shape...  18.5 us
    pallas_call x1, Pallas kernels, local(): pl.pallas_call(functools.partial(inward_kernel, pack), out_shape=jax.Shap...  17.7 us
    pallas_call x1, Pallas kernels, local(): pl.pallas_call(functools.partial(outward_kernel, pack, fields), out_shape...  13.8 us
    unnamed x6, local copies, waits for them, and re-layouts  2.03 us
    cos x1, other arithmetic, wave_tables(): jnp.cos(inner)  1.28 us

profile of v4, /device:TPU:0, one launch (start us, length us, event | category | flops | bytes accessed | tf_op | source)
XLA Modules:
  0.0 58.3 jit_solution(14037290833653792910)
XLA Ops:
  0.0 0.8 %reshape.236 = s32[80,32]{1,0:T(8,128)S(1)} reshape(s32[2560]{0:T(1024)} %param.10) | data formatting | bytes 20480 | tf_op jit(solution)/shard_map/reshape | solution.py:467
  0.8 0.1 select_reduce_fusion.lengths
  0.9 0.0 copy-start.1
  0.9 0.7 %convert_element_type.28 = f32[8]{0:T(128)S(1)} convert(s32[8]{0:T(128)} %deal.1) | non-fusion elementwise | flops 8 | bytes 64 | tf_op jit(solution)/shard_map/convert_element_type | solution.py:230
  1.6 0.1 iota_multiply_fusion
  1.7 1.3 %fusion.5 = (f32[80,8,128]{2,1,0:T(8,128)S(1)}, f32[80,8,128]{2,1,0:T(8,128)S(1)}) fusion(f32[80]{0:T(128)S(1)} %convert_element_type.29, f32[8,128]{1,0:T(8,128)S(1)} %iota_multiply_fusion), kind=kLoop, calls=%fused_computation.7 | loop fusion | flops 491520 | bytes 659776 | tf_op jit(solution)/shard_map/cos | solution.py:242
  2.9 0.7 %broadcast_multiply_fusion = f32[8]{0:T(128)S(1)} fusion(s32[8]{0:T(128)} %deal.1), kind=kLoop, calls=%fused_computation.22 | loop fusion | flops 16 | bytes 64 | tf_op jit(solution)/shard_map/mul | solution.py:233
  3.6 0.1 fusion.11
  3.7 0.1 copy.16
  3.8 0.1 broadcast_in_dim.18
  4.0 0.1 copy.17
  4.0 0.1 broadcast_in_dim.19
  4.2 0.0 copy-start
  4.2 1.2 %pad_maximum_fusion.table_ref = f32[80,32,128]{2,1,0:T(8,128)} fusion(f32[80,8,128]{2,1,0:T(8,128)S(1)} %broadcast_in_dim.19, f32[80,8,128]{2,1,0:T(8,128)S(1)} %broadcast_in_dim.18, f32[80,8,128]{2,1,0:T(8,128)S(1)} %get-tuple-element.6, f32[80,8,128]{2,1,0:T(8,128)S(1)} %get-tuple-element.5), kind=kLoop, calls=%fused_computation | loop fusion | flops 983040 | bytes 2621440 | tf_op jit(solution)/shard_map/concatenate | solution.py:240
  5.4 0.1 multiply_sine_fusion
  5.5 0.1 reshape.240
  5.6 0.0 copy-done.1
  5.6 0.7 %copy.18.weight_ref = f32[80,1,1]{2,1,0:T(1,128)} copy(f32[80,1,1]{0,2,1:T(1,128)S(1)} %bitcast_multiply_fusion) | data formatting | bytes 640 | tf_op jit(solution)/shard_map/div | solution.py:256
  6.3 0.0 copy-done
  6.3 0.6 %copy.19.pattern_ref = s32[2,20,20]{2,1,0:T(8,128)} copy(s32[2,20,20]{2,0,1:T(2,128)S(1)} %copy-done) | data formatting | bytes 6400 | tf_op args[2]
  6.9 17.7 %shard_map.64.fourier_ref = bf16[4,40,128]{2,1,0:T(8,128)(2,1)} custom-call(s32[2,20,20]{2,1,0:T(8,128)} %copy.19.pattern_ref, bf16[2,2,8,320]{3,2,1,0:T(8,128)(2,1)} %spec_ref.1, bf16[2,320,2560]{2,1,0:T(8,128)(2,1)} %legendre_ref.3), custom_call_target="tpu_custom_call" | custom-call | tf_op jit(solution)/shard_map/pallas_call | solution.py:447
  24.6 18.5 %shard_map.65.rows_ref = bf16[4,40,128]{2,1,0:T(8,128)(2,1)} custom-call(s32[80]{0:T(128)} %copy-done.1, s32[8]{0:T(128)} %deal.1, bf16[4,40,128]{2,1,0:T(8,128)(2,1)} %shard_map.64.fourier_ref, bf16[8,8]{1,0:T(8,128)(2,1)} %mixing_ref.1, f32[80,32,128]{2,1,0:T(8,128)} %pad_maximum_fusion.table_ref, f32[80,1,1]{2,1,0:T(1,128)} %copy.18.weight_ref), custom_call_target="tpu_custom_call" | custom-call | tf_op jit(solution)/shard_map/pallas_call | solution.py:261
  43.1 13.8 %shard_map.66 = f32[2,16,320]{2,1,0:T(8,128)} custom-call(s32[2,20,20]{2,1,0:T(8,128)} %copy.19.pattern_ref, bf16[4,40,128]{2,1,0:T(8,128)(2,1)} %shard_map.65.rows_ref, bf16[2,320,2560]{2,1,0:T(8,128)(2,1)} %legendre_ref.3), custom_call_target="tpu_custom_call" | custom-call | tf_op jit(solution)/shard_map/pallas_call | solution.py:471
  56.9 1.4 %copy.21 = f32[2,2,8,320]{3,2,1,0:T(8,128)} copy(f32[2,2,8,320]{3,2,1,0:T(8,128)} %bitcast.3) | data formatting | bytes 81920
  (5 shorter events, 0.0 us)
Async XLA Ops:
  0.9 4.7 %copy-start.1 = (s32[80]{0:T(128)}, s32[80]{0:T(128)S(1)}, u32[]{:S(2)}) copy-start(s32[80]{0:T(128)S(1)} %select_reduce_fusion.lengths) | copy-start | bytes 964
  4.2 2.1 %copy-start = (s32[2,20,20]{2,0,1:T(2,128)S(1)}, s32[2,20,20]{2,0,1:T(2,128)}, u32[]{:S(2)}) copy-start(s32[2,20,20]{2,0,1:T(2,128)} %param.8) | copy-start | bytes 9604

commit v5 on v4

--- a/solution.py
+++ b/solution.py
@@ -291,6 +291,14 @@
 
 
 def greet():
+    expect(hail())
+
+
+def expect(total):
+    pl.semaphore_wait(pltpu.get_barrier_semaphore(), total)
+
+
+def hail():
     barrier = pltpu.get_barrier_semaphore()
     total = 0
     for axis in ("lat", "lev"):
@@ -299,7 +307,7 @@
                 barrier, inc=1, device_id={axis: peer}, device_id_type=pl.DeviceIdType.MESH
             )
             total += 1
-    pl.semaphore_wait(barrier, total)
+    return total
 
 
 def send(axis, sources, target, sems):
@@ -325,6 +333,7 @@
     devices = lev_count * lat_count
     lev_index, lat_index = lax.axis_index("lev"), lax.axis_index("lat")
     packed = half_lat // pack
+    greetings = hail()
     odd, masks = column_masks(pattern_ref, legendre_ref.shape[1])
     sums = []
     for slot in range(slots):
@@ -354,7 +363,7 @@
             leaving[device // lat_count, device % lat_count, :, at * BLK : (at + 1) * BLK] = (
                 turned[at, pl.ds(device, count, stride=devices), :].astype(jnp.bfloat16)
             )
-    greet()
+    expect(greetings)
     copies = send("lev", lambda peer: leaving.at[peer], arriving.at[lev_index], lev_sems)
     mine = lev_index * lat_count
     total = jnp.stack(

time: 58.8 us -> 57.7 us (0.981)
  Pallas kernels: 49.9 us -> 49.2 us
    pallas_call x1, Pallas kernels: 17.7 us -> 16.7 us  [local(): pl.pallas_call(functools.partial(inward_kernel, pack), out_shape=jax.Shap...]
where the time goes in v5:
time: 57.7 us; the launch traced here: 57.6 us
  Pallas kernels  49.2 us (85%)
  other arithmetic  4.18 us (7%)
  local copies, waits for them, and re-layouts  4.09 us (7%)
    pallas_call x1, Pallas kernels, rows_step(): pl.pallas_call(functools.partial(row_kernel, half_lat // pack), out_shape...  19 us
    pallas_call x1, Pallas kernels, local(): pl.pallas_call(functools.partial(inward_kernel, pack), out_shape=jax.Shap...  16.7 us
    pallas_call x1, Pallas kernels, local(): pl.pallas_call(functools.partial(outward_kernel, pack, fields), out_shape...  13.5 us
    unnamed x6, local copies, waits for them, and re-layouts  2.03 us
    cos x1, other arithmetic, wave_tables(): jnp.cos(inner)  1.28 us
    concatenate x1, other arithmetic, wave_tables(): jnp.concatenate([jnp.cos(inner), jnp.sin(inner), jnp.broadcast_to(jnp.cos...  1.15 us

profile of v5, /device:TPU:0, one launch (start us, length us, event | category | flops | bytes accessed | tf_op | source)
XLA Modules:
  0.0 57.6 jit_solution(2436505876136267609)
XLA Ops:
  0.0 0.8 %reshape.236 = s32[80,32]{1,0:T(8,128)S(1)} reshape(s32[2560]{0:T(1024)} %param.10) | data formatting | bytes 20480 | tf_op jit(solution)/shard_map/reshape | solution.py:476
  0.8 0.1 select_reduce_fusion.lengths
  0.9 0.0 copy-start.1
  0.9 0.7 %convert_element_type.28 = f32[8]{0:T(128)S(1)} convert(s32[8]{0:T(128)} %deal.1) | non-fusion elementwise | flops 8 | bytes 64 | tf_op jit(solution)/shard_map/convert_element_type | solution.py:230
  1.6 0.1 iota_multiply_fusion
  1.7 1.3 %fusion.5 = (f32[80,8,128]{2,1,0:T(8,128)S(1)}, f32[80,8,128]{2,1,0:T(8,128)S(1)}) fusion(f32[80]{0:T(128)S(1)} %convert_element_type.29, f32[8,128]{1,0:T(8,128)S(1)} %iota_multiply_fusion), kind=kLoop, calls=%fused_computation.7 | loop fusion | flops 491520 | bytes 659776 | tf_op jit(solution)/shard_map/cos | solution.py:242
  2.9 0.7 %broadcast_multiply_fusion = f32[8]{0:T(128)S(1)} fusion(s32[8]{0:T(128)} %deal.1), kind=kLoop, calls=%fused_computation.22 | loop fusion | flops 16 | bytes 64 | tf_op jit(solution)/shard_map/mul | solution.py:233
  3.6 0.1 fusion.11
  3.7 0.1 copy.16
  3.8 0.1 broadcast_in_dim.18
  4.0 0.1 copy.17
  4.0 0.1 broadcast_in_dim.19
  4.2 0.0 copy-start
  4.2 1.2 %pad_maximum_fusion.table_ref = f32[80,32,128]{2,1,0:T(8,128)} fusion(f32[80,8,128]{2,1,0:T(8,128)S(1)} %broadcast_in_dim.19, f32[80,8,128]{2,1,0:T(8,128)S(1)} %broadcast_in_dim.18, f32[80,8,128]{2,1,0:T(8,128)S(1)} %get-tuple-element.6, f32[80,8,128]{2,1,0:T(8,128)S(1)} %get-tuple-element.5), kind=kLoop, calls=%fused_computation | loop fusion | flops 983040 | bytes 2621440 | tf_op jit(solution)/shard_map/concatenate | solution.py:240
  5.4 0.1 multiply_sine_fusion
  5.5 0.1 reshape.240
  5.6 0.0 copy-done.1
  5.6 0.7 %copy.18.weight_ref = f32[80,1,1]{2,1,0:T(1,128)} copy(f32[80,1,1]{0,2,1:T(1,128)S(1)} %bitcast_multiply_fusion) | data formatting | bytes 640 | tf_op jit(solution)/shard_map/div | solution.py:256
  6.3 0.0 copy-done
  6.3 0.6 %copy.19.pattern_ref = s32[2,20,20]{2,1,0:T(8,128)} copy(s32[2,20,20]{2,0,1:T(2,128)S(1)} %copy-done) | data formatting | bytes 6400 | tf_op args[2]
  6.9 16.7 %shard_map.64.fourier_ref = bf16[4,40,128]{2,1,0:T(8,128)(2,1)} custom-call(s32[2,20,20]{2,1,0:T(8,128)} %copy.19.pattern_ref, bf16[2,2,8,320]{3,2,1,0:T(8,128)(2,1)} %spec_ref.1, bf16[2,320,2560]{2,1,0:T(8,128)(2,1)} %legendre_ref.3), custom_call_target="tpu_custom_call" | custom-call | tf_op jit(solution)/shard_map/pallas_call | solution.py:456
  23.6 19.0 %shard_map.65.rows_ref = bf16[4,40,128]{2,1,0:T(8,128)(2,1)} custom-call(s32[80]{0:T(128)} %copy-done.1, s32[8]{0:T(128)} %deal.1, bf16[4,40,128]{2,1,0:T(8,128)(2,1)} %shard_map.64.fourier_ref, bf16[8,8]{1,0:T(8,128)(2,1)} %mixing_ref.1, f32[80,32,128]{2,1,0:T(8,128)} %pad_maximum_fusion.table_ref, f32[80,1,1]{2,1,0:T(1,128)} %copy.18.weight_ref), custom_call_target="tpu_custom_call" | custom-call | tf_op jit(solution)/shard_map/pallas_call | solution.py:261
  42.6 13.5 %shard_map.66 = f32[2,16,320]{2,1,0:T(8,128)} custom-call(s32[2,20,20]{2,1,0:T(8,128)} %copy.19.pattern_ref, bf16[4,40,128]{2,1,0:T(8,128)(2,1)} %shard_map.65.rows_ref, bf16[2,320,2560]{2,1,0:T(8,128)(2,1)} %legendre_ref.3), custom_call_target="tpu_custom_call" | custom-call | tf_op jit(solution)/shard_map/pallas_call | solution.py:480
  56.1 1.4 %copy.21 = f32[2,2,8,320]{3,2,1,0:T(8,128)} copy(f32[2,2,8,320]{3,2,1,0:T(8,128)} %bitcast.3) | data formatting | bytes 81920
  (5 shorter events, 0.0 us)
Async XLA Ops:
  0.9 4.7 %copy-start.1 = (s32[80]{0:T(128)}, s32[80]{0:T(128)S(1)}, u32[]{:S(2)}) copy-start(s32[80]{0:T(128)S(1)} %select_reduce_fusion.lengths) | copy-start | bytes 964
  4.2 2.1 %copy-start = (s32[2,20,20]{2,0,1:T(2,128)S(1)}, s32[2,20,20]{2,0,1:T(2,128)}, u32[]{:S(2)}) copy-start(s32[2,20,20]{2,0,1:T(2,128)} %param.8) | copy-start | bytes 9604
